TPU v7x, 512 devices: a whole 4x8x8 slice. The times are simulated.
512 devices in a mesh: row: 16 (over y, core), col: 32 (over z, x).
Axes of the slice: x: 4, y: 8, z: 8, core: 2. Of those that a mesh axis runs over, the one named last changes fastest.
Arguments:
- snapshots: bfloat16 [64, 1536, 4096], P(None, 'row', 'col'), may hold values from -870 to 870
Outputs:
- q_blocks: float32 [64, 1536, 4096], P(None, 'row', 'col')
- r_factor: float32 [64, 64], replicated
All inputs are finite; a program needn't handle non-finite values.
Results may differ from a plain program's by a relative error of at most 0.0003.
Values may be sent and summed in bfloat16 or wider, within the bound.
No kernel may reach another device: no remote copies, remote signals or barrier semaphores. Data moves between devices by JAX's collectives and lax.ppermute only.
A program may use at most 64 MiB of HBM per device.

v0:
```python
import jax
import jax.numpy as jnp
from jax import lax
from jax.sharding import PartitionSpec as P

HALF = 16


def padded(array, sides, width):
    for axis, dim in sides:
        devices, length = (lax.axis_size(axis), array.shape[dim])
        up = [(i, (i + 1) % devices) for i in range(devices)]
        down = [(j, i) for i, j in up]
        last = lax.slice_in_dim(array, length - width, length, axis=dim)
        initial = lax.slice_in_dim(array, 0, width, axis=dim)
        before = lax.ppermute(last, axis, up)
        after = lax.ppermute(initial, axis, down)
        array = jnp.concatenate([before, array, after], axis=dim)
    return array


def band_matrix(length):
    sigma = HALF / 3.0
    offsets = jnp.arange(2 * HALF + 1, dtype=jnp.float32) - HALF
    total = jnp.sum(jnp.exp(-offsets * offsets / (2.0 * sigma * sigma)))
    outer = jnp.arange(length + 2 * HALF)[:, None]
    inner = jnp.arange(length)[None, :]
    spread = outer - inner
    shifted = (spread - HALF).astype(jnp.float32)
    inside = (spread >= 0) & (spread <= 2 * HALF)
    return jnp.where(inside, jnp.exp(-shifted * shifted / (2.0 * sigma * sigma)) / total, 0.0)


def filter_columns(field):
    width = field.shape[2] - 2 * HALF
    return jnp.einsum("src,cd->srd", field, band_matrix(width), precision=lax.Precision.HIGHEST)


def filter_rows(field):
    height = field.shape[1] - 2 * HALF
    return jnp.einsum("src,rq->sqc", field, band_matrix(height), precision=lax.Precision.HIGHEST)


def local(snapshots):
    count, height, width = snapshots.shape
    extended = padded(snapshots, (("row", 1), ("col", 2)), HALF)
    filtered = filter_rows(filter_columns(extended.astype(jnp.float32)))
    points = height * width * lax.axis_size("row") * lax.axis_size("col")
    flat_field = filtered.reshape(count, height * width)
    local_gram = jnp.dot(flat_field, flat_field.T, precision=lax.Precision.HIGHEST) / points
    gram = lax.psum(local_gram, "row")
    gram = lax.psum(gram, "col")
    upper = jnp.linalg.cholesky(gram).T
    basis = lax.linalg.triangular_solve(upper.T, flat_field, left_side=True, lower=True)
    return (basis.reshape(count, height, width), upper)


def solution(mesh):
    return jax.shard_map(
        local,
        mesh=mesh,
        in_specs=(P(None, "row", "col"),),
        out_specs=(P(None, "row", "col"), P()),
        check_vma=False,
    )
```

profile of v0, /device:TPU:32, one launch (start us, length us, event | category | flops | bytes accessed | tf_op | source)
XLA Modules:
  0.0 261.6 jit_solution(15166263023438146916)
XLA Ops:
  0.6 1.1 fusion.77
  1.7 0.0 collective-permute-start.1
  1.7 0.5 collective-permute-start
  2.2 3.1 %copy.30 = bf16[64,96,128]{1,2,0:T(8,128)(2,1)S(1)} copy(bf16[64,96,128]{2,1,0:T(8,128)(2,1)} %param.1) | data formatting | bytes 3145728 | tf_op args[0]
  5.4 0.3 collective-permute-done.1
  5.6 1.7 copy.31
  7.3 1.4 collective-permute-done
  8.8 1.8 copy.29
  10.5 0.0 copy-start
  10.5 0.0 copy-start.1
  10.5 1.8 pad_maximum_fusion.2
  12.4 3.4 %collective-permute-start.2 = (bf16[64,128,16]{1,2,0:T(8,128)(2,1)S(1)}, bf16[64,128,16]{1,2,0:T(8,128)(2,1)S(1)}, u32[]{:S(2)}, u32[]{:S(2)}) collective-permute-start(bf16[64,128,16]{1,2,0:T(8,128)(2,1)S(1)} %get-tuple-element.10), channel_id=1, source_target_pairs={{0,1},{1,2},{2,3},{3,4},{4,5},{5,6},{6,7},{7,8},{8,9},{9,10},{10,1... | collective-permute-start | bytes 786440 | tf_op jit(solution)/shard_map/ppermute | solution.py:16
  15.8 11.7 %collective-permute-start.3 = (bf16[64,128,16]{1,2,0:T(8,128)(2,1)S(1)}, bf16[64,128,16]{1,2,0:T(8,128)(2,1)S(1)}, u32[]{:S(2)}, u32[]{:S(2)}) collective-permute-start(bf16[64,128,16]{1,2,0:T(8,128)(2,1)S(1)} %get-tuple-element.11), channel_id=1, source_target_pairs={{1,0},{2,1},{3,2},{4,3},{5,4},{6,5},{7,6},{8,7},{9,8},{10,9},{11,1... | collective-permute-start | bytes 786440 | tf_op jit(solution)/shard_map/ppermute | solution.py:17
  27.5 0.6 fusion.65
  28.1 4.5 %collective-permute-done.2 = bf16[64,128,16]{1,2,0:T(8,128)(2,1)S(1)} collective-permute-done((bf16[64,128,16]{1,2,0:T(8,128)(2,1)S(1)}, bf16[64,128,16]{1,2,0:T(8,128)(2,1)S(1)}, u32[]{:S(2)}, u32[]{:S(2)}) %collective-permute-start.2) | collective-permute-done | bytes 262176 | tf_op jit(solution)/shard_map/ppermute | solution.py:16
  32.6 1.2 collective-permute-done.3
  33.8 0.0 copy-done
  33.8 0.0 copy-done.1
  33.8 7.8 %fusion.5 = f32[64,128,128]{2,1,0:T(8,128)S(1)} fusion(bf16[64,128,16]{1,2,0:T(8,128)(2,1)S(1)} %collective-permute-done.3, bf16[64,16,128]{1,2,0:T(8,128)(2,1)S(1)} %copy-done, bf16[64,96,128]{1,2,0:T(8,128)(2,1)S(1)} %copy.30, bf16[64,16,128]{1,2,0:T(8,128)(2,1)S(1)} %copy-done.1, bf16[64,128,16]{1,2,0:T(8,128)(2,1)S(1)} %collective-permute-done.2, f32[]{:T(128)} %fusion.65), kind=kOutput, calls=%fused_computation.6 | convolution fusion | flops 2026598400 | bytes 6815748 | tf_op jit(solution)/shard_map/src,cd->srd/dot_general | solution.py:36
  41.5 3.7 %fusion.39 = f32[96,64,128]{2,0,1:T(8,128)S(1)} fusion(f32[64,128,128]{2,1,0:T(8,128)S(1)} %fusion.5, f32[]{:T(128)} %fusion.65), kind=kOutput, calls=%fused_computation.39 | convolution fusion | flops 1208094720 | bytes 7340036 | tf_op jit(solution)/shard_map/src,rq->sqc/dot_general | solution.py:41
  45.3 6.1 %fusion.18 = f32[64,64]{0,1:T(8,128)S(1)} fusion(f32[64,96,128]{2,1,0:T(8,128)S(1)} %bitcast.38), kind=kOutput, calls=%fused_computation.17 | convolution fusion | flops 603983872 | bytes 3162112 | tf_op jit(solution)/shard_map/dot_general | solution.py:50
  51.4 45.7 %psum.14 = f32[64,64]{0,1:T(8,128)S(1)} all-reduce(f32[64,64]{0,1:T(8,128)S(1)} %fusion.18), channel_id=1, replica_groups=mesh['row'=16,'col'=32] {'row'}, use_global_device_ids=true, to_apply=%region_1.2 | all-reduce | flops 4096 | bytes 32768 | tf_op jit(solution)/shard_map/psum | solution.py:51
  97.2 143.4 %psum.15 = f32[64,64]{0,1:T(8,128)S(1)} all-reduce(f32[64,64]{0,1:T(8,128)S(1)} %psum.14), channel_id=1, replica_groups=mesh['row'=16,'col'=32] {'col'}, use_global_device_ids=true, to_apply=%region_2.3 | all-reduce | flops 4096 | bytes 32768 | tf_op jit(solution)/shard_map/psum | solution.py:52
  240.6 0.1 copy.35
  240.7 5.8 %cholesky.16 = f32[64,64]{1,0:T(8,128)S(1)} custom-call(f32[64,64]{1,0:T(8,128)S(1)} %fusion.55), custom_call_target="Cholesky" | custom-call | tf_op jit(solution)/shard_map/jit(cholesky)/cholesky | solution.py:53
  246.6 0.6 compare_reduce_fusion
  247.2 0.7 fusion.56
  247.9 0.7 copy.39
  248.6 4.9 %custom-call.6 = f32[1,64,64]{1,2,0:T(8,128)S(1)} custom-call(f32[1,64,64]{2,1,0:T(8,128)S(1)} %get-tuple-element.15), custom_call_target="InvertDiagBlocksLowerTriangular" | custom-call | tf_op jit(solution)/shard_map/triangular_solve | solution.py:54
  253.5 4.6 %fusion = f32[64,96,128]{2,0,1:T(8,128)S(1)} fusion(f32[1,64,64]{1,2,0:T(8,128)S(1)} %custom-call.6, f32[8,8,96,128]{3,2,1,0:T(8,128)S(1)} %bitcast.39), kind=kOutput, calls=%fused_computation.1 | convolution fusion | flops 603979776 | bytes 6307840 | tf_op jit(solution)/shard_map/triangular_solve | solution.py:54
  258.1 3.5 %copy.38 = f32[64,96,128]{2,1,0:T(8,128)} copy(f32[64,96,128]{2,0,1:T(8,128)S(1)} %fusion) | data formatting | bytes 6291456
  (2 shorter events, 0.0 us)
Async XLA Ops:
  1.7 3.9 %collective-permute-start.1 = (bf16[64,16,128]{2,1,0:T(8,128)(2,1)S(1)}, bf16[64,16,128]{2,1,0:T(8,128)(2,1)S(1)}, u32[]{:S(2)}, u32[]{:S(2)}) collective-permute-start(bf16[64,16,128]{2,1,0:T(8,128)(2,1)S(1)} %get-tuple-element.13), channel_id=1, source_target_pairs={{32,0},{64,32},{96,64},{128,96},{160,128},{192,160},{224,192},{256... | collective-permute-start | bytes 786440 | tf_op jit(solution)/shard_map/ppermute | solution.py:17
  1.7 7.0 %collective-permute-start = (bf16[64,16,128]{2,1,0:T(8,128)(2,1)S(1)}, bf16[64,16,128]{2,1,0:T(8,128)(2,1)S(1)}, u32[]{:S(2)}, u32[]{:S(2)}) collective-permute-start(bf16[64,16,128]{2,1,0:T(8,128)(2,1)S(1)} %get-tuple-element.12), channel_id=1, source_target_pairs={{0,32},{32,64},{64,96},{96,128},{128,160},{160,192},{192,224},{224... | collective-permute-start | bytes 786440 | tf_op jit(solution)/shard_map/ppermute | solution.py:16
  10.5 23.2 %copy-start = (bf16[64,16,128]{1,2,0:T(8,128)(2,1)S(1)}, bf16[64,16,128]{1,2,0:T(8,128)(2,1)}, u32[]{:S(2)}) copy-start(bf16[64,16,128]{1,2,0:T(8,128)(2,1)} %copy.31) | copy-start | bytes 786436
  10.5 23.2 %copy-start.1 = (bf16[64,16,128]{1,2,0:T(8,128)(2,1)S(1)}, bf16[64,16,128]{1,2,0:T(8,128)(2,1)}, u32[]{:S(2)}) copy-start(bf16[64,16,128]{1,2,0:T(8,128)(2,1)} %copy.29) | copy-start | bytes 786436
  12.4 20.2 %collective-permute-start.2 = (bf16[64,128,16]{1,2,0:T(8,128)(2,1)S(1)}, bf16[64,128,16]{1,2,0:T(8,128)(2,1)S(1)}, u32[]{:S(2)}, u32[]{:S(2)}) collective-permute-start(bf16[64,128,16]{1,2,0:T(8,128)(2,1)S(1)} %get-tuple-element.10), channel_id=1, source_target_pairs={{0,1},{1,2},{2,3},{3,4},{4,5},{5,6},{6,7},{7,8},{8,9},{9,10},{10,1... | collective-permute-start | bytes 786440 | tf_op jit(solution)/shard_map/ppermute | solution.py:16
  15.8 18.0 %collective-permute-start.3 = (bf16[64,128,16]{1,2,0:T(8,128)(2,1)S(1)}, bf16[64,128,16]{1,2,0:T(8,128)(2,1)S(1)}, u32[]{:S(2)}, u32[]{:S(2)}) collective-permute-start(bf16[64,128,16]{1,2,0:T(8,128)(2,1)S(1)} %get-tuple-element.11), channel_id=1, source_target_pairs={{1,0},{2,1},{3,2},{4,3},{5,4},{6,5},{7,6},{8,7},{9,8},{10,9},{11,1... | collective-permute-start | bytes 786440 | tf_op jit(solution)/shard_map/ppermute | solution.py:17
where the time goes:
time: 262 us
  blocking collectives  189 us (72%)
  matrix products  22.2 us (8%)
  starting transfers between devices  15.6 us (6%)
  other arithmetic  14.5 us (6%)
  local copies, waits for them, and re-layouts  11.9 us (5%)
  waiting for transfers between devices  7.39 us (3%)
    psum x1, blocking collectives, local(): gram = lax.psum(gram, 'col')  143 us
    psum x1, blocking collectives, local(): gram = lax.psum(local_gram, 'row')  45.7 us
    ppermute x2, starting transfers between devices, padded(): after = lax.ppermute(initial, axis, down)  11.7 us
    dot_general x1, matrix products, filter_columns(): jnp.einsum('src,cd->srd', field, band_matrix(width), precision=lax.Precis...  7.76 us
    unnamed x7, local copies, waits for them, and re-layouts  7.3 us
    another operation x3, other arithmetic, local(): upper = jnp.linalg.cholesky(gram).T  6.52 us
    dot_general x1, matrix products, local(): jnp.dot(flat_field, flat_field.T, precision=lax.Precision.HIGHEST) / points  6.13 us
    ppermute x2, waiting for transfers between devices, padded(): before = lax.ppermute(last, axis, up)  5.94 us
  transfers between devices with their start and end apart: 4, of which 4 were waited for; matrix products, arithmetic and copies ran while one was open for 2% of the time, Pallas kernels for 0%

commit v1 on v0

--- a/solution.py
+++ b/solution.py
@@ -33,12 +33,42 @@
 
 def filter_columns(field):
     width = field.shape[2] - 2 * HALF
-    return jnp.einsum("src,cd->srd", field, band_matrix(width), precision=lax.Precision.HIGHEST)
+    return jnp.einsum("src,cd->srd", field, band_matrix(width), precision=lax.Precision.HIGH)
 
 
 def filter_rows(field):
     height = field.shape[1] - 2 * HALF
-    return jnp.einsum("src,rq->sqc", field, band_matrix(height), precision=lax.Precision.HIGHEST)
+    return jnp.einsum("src,rq->sqc", field, band_matrix(height), precision=lax.Precision.HIGH)
+
+
+def pack(gram):
+    half = gram.shape[0] // 2
+    first, second = gram[:half, :half], gram[half:, half:]
+    row = lax.broadcasted_iota(jnp.int32, (half, half), 0)
+    col = lax.broadcasted_iota(jnp.int32, (half, half), 1)
+    mixed = jnp.where(row >= col, first, second)
+    diagonal = jnp.sum(jnp.where(row == col, second, 0.0), axis=0)
+    diagonal = jnp.pad(diagonal, (0, half))[None]
+    top = jnp.concatenate([gram[half:, :half], mixed], axis=1)
+    return jnp.concatenate([top, diagonal, jnp.zeros_like(diagonal)], axis=0)
+
+
+def unpack(packed):
+    half = packed.shape[1] // 2
+    cross, mixed, diagonal = packed[:half, :half], packed[:half, half:], packed[half, :half]
+    row = lax.broadcasted_iota(jnp.int32, (half, half), 0)
+    col = lax.broadcasted_iota(jnp.int32, (half, half), 1)
+    first = jnp.where(row >= col, mixed, mixed.T)
+    second = jnp.where(row < col, mixed, mixed.T)
+    second = jnp.where(row == col, diagonal[None], second)
+    return jnp.concatenate(
+        [jnp.concatenate([first, cross.T], axis=1), jnp.concatenate([cross, second], axis=1)], axis=0
+    )
+
+
+def summed(array, axis):
+    copies = jnp.broadcast_to(array[None], (lax.axis_size(axis),) + array.shape)
+    return lax.all_to_all(copies, axis, 0, 0).sum(0)
 
 
 def local(snapshots):
@@ -47,11 +77,13 @@
     filtered = filter_rows(filter_columns(extended.astype(jnp.float32)))
     points = height * width * lax.axis_size("row") * lax.axis_size("col")
     flat_field = filtered.reshape(count, height * width)
-    local_gram = jnp.dot(flat_field, flat_field.T, precision=lax.Precision.HIGHEST) / points
-    gram = lax.psum(local_gram, "row")
-    gram = lax.psum(gram, "col")
-    upper = jnp.linalg.cholesky(gram).T
-    basis = lax.linalg.triangular_solve(upper.T, flat_field, left_side=True, lower=True)
+    local_gram = jnp.dot(flat_field, flat_field.T, precision=lax.Precision.HIGH) / points
+    total = pack(local_gram).reshape(-1)
+    total = summed(summed(total, "row"), "col")
+    gram = unpack(total.reshape(count // 2 + 2, count))
+    upper = jnp.linalg.cholesky(gram, symmetrize_input=False).T
+    inverse = lax.linalg.triangular_solve(upper.T, jnp.eye(count, dtype=jnp.float32), left_side=True, lower=True)
+    basis = jnp.dot(inverse, flat_field, precision=lax.Precision.HIGH)
     return (basis.reshape(count, height, width), upper)
 
 

time: 262 us -> 106 us (0.40)
  the two profiles are of different devices: /device:TPU:32 before, /device:TPU:1 now
where the time goes in v1:
time: 106 us; the launch traced here: 105 us
  blocking collectives  37.9 us (36%)
  starting transfers between devices  18.4 us (17%)
  matrix products  17.6 us (17%)
  other arithmetic  15.1 us (14%)
  local copies, waits for them, and re-layouts  12.5 us (12%)
  waiting for transfers between devices  3.15 us (3%)
    all_to_all x2, blocking collectives, summed(): return lax.all_to_all(copies, axis, 0, 0).sum(0)  37.9 us
    ppermute x2, starting transfers between devices, padded(): after = lax.ppermute(initial, axis, down)  13.8 us
    unnamed x8, local copies, waits for them, and re-layouts  7.37 us
    dot_general x1, matrix products, filter_columns(): jnp.einsum('src,cd->srd', field, band_matrix(width), precision=lax.Precis...  6.69 us
    another operation x3, other arithmetic, local(): upper = jnp.linalg.cholesky(gram, symmetrize_input=False).T  6.53 us
    dot_general x1, matrix products, local(): jnp.dot(flat_field, flat_field.T, precision=lax.Precision.HIGH) / points  5.08 us
    another operation x1, other arithmetic, local(): lax.linalg.triangular_solve(upper.T, jnp.eye(count, dtype=jnp.float32), l...  4.9 us
    ppermute x2, starting transfers between devices, padded(): before = lax.ppermute(last, axis, up)  4.61 us
  transfers between devices with their start and end apart: 4, of which 2 were waited for; matrix products, arithmetic and copies ran while one was open for 5% of the time, Pallas kernels for 0%

profile of v1, /device:TPU:1, one launch (start us, length us, event | category | flops | bytes accessed | tf_op | source)
XLA Modules:
  0.0 105.4 jit_solution(1325105511853042702)
XLA Ops:
  0.6 1.1 %fusion.77 = (bf16[64,16,128]{2,1,0:T(8,128)(2,1)S(1)}, bf16[64,16,128]{2,1,0:T(8,128)(2,1)S(1)}) fusion(bf16[64,96,128]{2,1,0:T(8,128)(2,1)} %param.1), kind=kLoop, calls=%fused_computation.94 | loop fusion | bytes 1048576 | tf_op jit(solution)/shard_map/slice | solution.py:14
  1.7 2.7 %collective-permute-start = (bf16[64,16,128]{2,1,0:T(8,128)(2,1)S(1)}, bf16[64,16,128]{2,1,0:T(8,128)(2,1)S(1)}, u32[]{:S(2)}, u32[]{:S(2)}) collective-permute-start(bf16[64,16,128]{2,1,0:T(8,128)(2,1)S(1)} %get-tuple-element.16), channel_id=1, source_target_pairs={{0,32},{32,64},{64,96},{96,128},{128,160},{160,192},{192,224},{224... | collective-permute-start | bytes 786440 | tf_op jit(solution)/shard_map/ppermute | solution.py:16
  4.4 4.2 %collective-permute-start.1 = (bf16[64,16,128]{2,1,0:T(8,128)(2,1)S(1)}, bf16[64,16,128]{2,1,0:T(8,128)(2,1)S(1)}, u32[]{:S(2)}, u32[]{:S(2)}) collective-permute-start(bf16[64,16,128]{2,1,0:T(8,128)(2,1)S(1)} %get-tuple-element.17), channel_id=1, source_target_pairs={{32,0},{64,32},{96,64},{128,96},{160,128},{192,160},{224,192},{256... | collective-permute-start | bytes 786440 | tf_op jit(solution)/shard_map/ppermute | solution.py:17
  8.6 3.1 %copy.52 = bf16[64,96,128]{1,2,0:T(8,128)(2,1)S(1)} copy(bf16[64,96,128]{2,1,0:T(8,128)(2,1)} %param.1) | data formatting | bytes 3145728 | tf_op args[0]
  11.7 0.0 collective-permute-done
  11.7 1.8 %copy.51 = bf16[64,16,128]{1,2,0:T(8,128)(2,1)} copy(bf16[64,16,128]{2,1,0:T(8,128)(2,1)S(1)} %collective-permute-done) | data formatting | bytes 524288 | tf_op jit(solution)/shard_map/ppermute | solution.py:16
  13.5 0.0 collective-permute-done.1
  13.5 1.7 %copy.53 = bf16[64,16,128]{1,2,0:T(8,128)(2,1)} copy(bf16[64,16,128]{2,1,0:T(8,128)(2,1)S(1)} %collective-permute-done.1) | data formatting | bytes 524288 | tf_op jit(solution)/shard_map/ppermute | solution.py:17
  15.2 0.0 copy-start
  15.2 0.0 copy-start.1
  15.2 1.8 %pad_maximum_fusion.2 = (bf16[64,128,16]{1,2,0:T(8,128)(2,1)S(1)}, bf16[64,128,16]{1,2,0:T(8,128)(2,1)S(1)}) fusion(bf16[64,16,128]{1,2,0:T(8,128)(2,1)} %copy.53, bf16[64,96,128]{1,2,0:T(8,128)(2,1)S(1)} %copy.52, bf16[64,16,128]{1,2,0:T(8,128)(2,1)} %copy.51), kind=kLoop, calls=%fused_computation.21 | loop fusion | flops 1572864 | bytes 2621440 | tf_op jit(solution)/shard_map/slice | solution.py:14
  17.1 1.9 %collective-permute-start.2 = (bf16[64,128,16]{1,2,0:T(8,128)(2,1)S(1)}, bf16[64,128,16]{1,2,0:T(8,128)(2,1)S(1)}, u32[]{:S(2)}, u32[]{:S(2)}) collective-permute-start(bf16[64,128,16]{1,2,0:T(8,128)(2,1)S(1)} %get-tuple-element.14), channel_id=1, source_target_pairs={{0,1},{1,2},{2,3},{3,4},{4,5},{5,6},{6,7},{7,8},{8,9},{9,10},{10,1... | collective-permute-start | bytes 786440 | tf_op jit(solution)/shard_map/ppermute | solution.py:16
  19.0 9.6 %collective-permute-start.3 = (bf16[64,128,16]{1,2,0:T(8,128)(2,1)S(1)}, bf16[64,128,16]{1,2,0:T(8,128)(2,1)S(1)}, u32[]{:S(2)}, u32[]{:S(2)}) collective-permute-start(bf16[64,128,16]{1,2,0:T(8,128)(2,1)S(1)} %get-tuple-element.15), channel_id=1, source_target_pairs={{1,0},{2,1},{3,2},{4,3},{5,4},{6,5},{7,6},{8,7},{9,8},{10,9},{11,1... | collective-permute-start | bytes 786440 | tf_op jit(solution)/shard_map/ppermute | solution.py:17
  28.6 0.1 pad.12.clone
  28.6 0.6 fusion.65
  29.3 2.2 %collective-permute-done.2 = bf16[64,128,16]{1,2,0:T(8,128)(2,1)S(1)} collective-permute-done((bf16[64,128,16]{1,2,0:T(8,128)(2,1)S(1)}, bf16[64,128,16]{1,2,0:T(8,128)(2,1)S(1)}, u32[]{:S(2)}, u32[]{:S(2)}) %collective-permute-start.2) | collective-permute-done | bytes 262176 | tf_op jit(solution)/shard_map/ppermute | solution.py:16
  31.5 0.9 collective-permute-done.3
  32.4 0.0 copy-done
  32.4 0.0 copy-done.1
  32.4 6.7 %fusion.5 = f32[64,128,128]{2,1,0:T(8,128)S(1)} fusion(bf16[64,128,16]{1,2,0:T(8,128)(2,1)S(1)} %collective-permute-done.3, bf16[64,16,128]{1,2,0:T(8,128)(2,1)S(1)} %copy-done.1, bf16[64,96,128]{1,2,0:T(8,128)(2,1)S(1)} %copy.52, bf16[64,16,128]{1,2,0:T(8,128)(2,1)S(1)} %copy-done, bf16[64,128,16]{1,2,0:T(8,128)(2,1)S(1)} %collective-permute-done.2, f32[]{:T(128)} %fusion.65), kind=kOutput, calls=%fused_computation.6 | convolution fusion | flops 1019965440 | bytes 6815748 | tf_op jit(solution)/shard_map/src,cd->srd/dot_general | solution.py:36
  39.1 2.3 %fusion.39 = f32[96,64,128]{2,0,1:T(8,128)S(1)} fusion(f32[64,128,128]{2,1,0:T(8,128)S(1)} %fusion.5, f32[]{:T(128)} %fusion.65), kind=kOutput, calls=%fused_computation.40 | convolution fusion | flops 604114944 | bytes 7340036 | tf_op jit(solution)/shard_map/src,rq->sqc/dot_general | solution.py:41
  41.4 5.1 %fusion.18 = f32[64,64]{1,0:T(8,128)S(1)} fusion(f32[64,96,128]{2,1,0:T(8,128)S(1)} %bitcast.46), kind=kOutput, calls=%fused_computation.18 | convolution fusion | flops 301993984 | bytes 3162112 | tf_op jit(solution)/shard_map/dot_general | solution.py:80
  46.5 0.1 fusion.78
  46.6 0.1 maximum_maximum_fusion.1
  46.7 0.1 broadcast_in_dim.52
  46.8 0.1 broadcast_in_dim.53
  46.8 18.1 %all_to_all.12 = f32[16,1,2176]{2,1,0:T(1,128)S(1)} all-to-all(f32[16,1,2176]{2,1,0:T(1,128)S(1)} %broadcast_in_dim.53), channel_id=1, replica_groups=mesh['row'=16,'col'=32] {'row'}, dimensions={0} | all-to-all | bytes 278528 | tf_op jit(solution)/shard_map/all_to_all | solution.py:71
  64.9 0.1 reduce_sum.42
  65.0 0.1 broadcast_in_dim.54
  65.2 19.8 %all_to_all.13 = f32[32,1,2176]{2,1,0:T(1,128)S(1)} all-to-all(f32[32,1,2176]{2,1,0:T(1,128)S(1)} %broadcast_in_dim.54), channel_id=1, replica_groups=mesh['row'=16,'col'=32] {'col'}, dimensions={0} | all-to-all | bytes 557056 | tf_op jit(solution)/shard_map/all_to_all | solution.py:71
  85.0 0.2 reduce_sum.43
  85.2 0.1 reshape.35
  85.3 0.1 slice.53
  85.3 0.1 copy.58
  85.4 0.1 bitcast_select_fusion.1
  85.5 0.1 copy.66
  85.6 0.1 maximum_maximum_fusion
  85.6 5.9 %cholesky.17 = f32[64,64]{1,0:T(8,128)S(1)} custom-call(f32[64,64]{1,0:T(8,128)S(1)} %maximum_maximum_fusion), custom_call_target="Cholesky" | custom-call | tf_op jit(solution)/shard_map/jit(cholesky)/cholesky | solution.py:84
  91.5 0.6 compare_reduce_fusion
  92.2 0.7 fusion.55
  92.8 4.9 %custom-call.6 = f32[1,64,64]{1,2,0:T(8,128)S(1)} custom-call(f32[1,64,64]{2,1,0:T(8,128)S(1)} %get-tuple-element.21), custom_call_target="InvertDiagBlocksLowerTriangular" | custom-call | tf_op jit(solution)/shard_map/triangular_solve | solution.py:85
  97.7 0.2 convolution_bitcast_fusion
  98.0 3.3 %fusion = f32[64,96,128]{2,0,1:T(8,128)S(1)} fusion(f32[64,64,1]{1,0,2:T(8,128)S(1)} %convolution_bitcast_fusion, f32[8,8,96,128]{3,2,1,0:T(8,128)S(1)} %bitcast.47), kind=kOutput, calls=%fused_computation.1 | convolution fusion | flops 301989888 | bytes 6307840 | tf_op jit(solution)/shard_map/dot_general | solution.py:86
  101.3 3.5 %copy.62 = f32[64,96,128]{2,1,0:T(8,128)} copy(f32[64,96,128]{2,0,1:T(8,128)S(1)} %fusion) | data formatting | bytes 6291456
  104.7 0.7 copy.63
  (3 shorter events, 0.0 us)
Async XLA Ops:
  1.7 10.0 %collective-permute-start = (bf16[64,16,128]{2,1,0:T(8,128)(2,1)S(1)}, bf16[64,16,128]{2,1,0:T(8,128)(2,1)S(1)}, u32[]{:S(2)}, u32[]{:S(2)}) collective-permute-start(bf16[64,16,128]{2,1,0:T(8,128)(2,1)S(1)} %get-tuple-element.16), channel_id=1, source_target_pairs={{0,32},{32,64},{64,96},{96,128},{128,160},{160,192},{192,224},{224... | collective-permute-start | bytes 786440 | tf_op jit(solution)/shard_map/ppermute | solution.py:16
  4.4 9.1 %collective-permute-start.1 = (bf16[64,16,128]{2,1,0:T(8,128)(2,1)S(1)}, bf16[64,16,128]{2,1,0:T(8,128)(2,1)S(1)}, u32[]{:S(2)}, u32[]{:S(2)}) collective-permute-start(bf16[64,16,128]{2,1,0:T(8,128)(2,1)S(1)} %get-tuple-element.17), channel_id=1, source_target_pairs={{32,0},{64,32},{96,64},{128,96},{160,128},{192,160},{224,192},{256... | collective-permute-start | bytes 786440 | tf_op jit(solution)/shard_map/ppermute | solution.py:17
  15.2 17.2 %copy-start = (bf16[64,16,128]{1,2,0:T(8,128)(2,1)S(1)}, bf16[64,16,128]{1,2,0:T(8,128)(2,1)}, u32[]{:S(2)}) copy-start(bf16[64,16,128]{1,2,0:T(8,128)(2,1)} %copy.51) | copy-start | bytes 786436
  15.2 17.2 %copy-start.1 = (bf16[64,16,128]{1,2,0:T(8,128)(2,1)S(1)}, bf16[64,16,128]{1,2,0:T(8,128)(2,1)}, u32[]{:S(2)}) copy-start(bf16[64,16,128]{1,2,0:T(8,128)(2,1)} %copy.53) | copy-start | bytes 786436
  17.1 14.4 %collective-permute-start.2 = (bf16[64,128,16]{1,2,0:T(8,128)(2,1)S(1)}, bf16[64,128,16]{1,2,0:T(8,128)(2,1)S(1)}, u32[]{:S(2)}, u32[]{:S(2)}) collective-permute-start(bf16[64,128,16]{1,2,0:T(8,128)(2,1)S(1)} %get-tuple-element.14), channel_id=1, source_target_pairs={{0,1},{1,2},{2,3},{3,4},{4,5},{5,6},{6,7},{7,8},{8,9},{9,10},{10,1... | collective-permute-start | bytes 786440 | tf_op jit(solution)/shard_map/ppermute | solution.py:16
  19.0 13.4 %collective-permute-start.3 = (bf16[64,128,16]{1,2,0:T(8,128)(2,1)S(1)}, bf16[64,128,16]{1,2,0:T(8,128)(2,1)S(1)}, u32[]{:S(2)}, u32[]{:S(2)}) collective-permute-start(bf16[64,128,16]{1,2,0:T(8,128)(2,1)S(1)} %get-tuple-element.15), channel_id=1, source_target_pairs={{1,0},{2,1},{3,2},{4,3},{5,4},{6,5},{7,6},{8,7},{9,8},{10,9},{11,1... | collective-permute-start | bytes 786440 | tf_op jit(solution)/shard_map/ppermute | solution.py:17

commit v2 on v1

v2 whole, which is shorter than its diff:
```python
import functools
import jax
import jax.numpy as jnp
import numpy as np
from jax import lax
from jax.experimental import pallas as pl
from jax.experimental.pallas import tpu as pltpu
from jax.sharding import PartitionSpec as P

HALF = 16
TAPS = 2 * HALF + 1
BF16, F32 = jnp.bfloat16, jnp.float32
STEP = 48


def band(length):
    sigma = HALF / 3.0
    offsets = np.arange(TAPS) - HALF
    weights = np.exp(-offsets * offsets / (2.0 * sigma * sigma))
    weights = weights / weights.sum()
    result = np.zeros((length + 2 * HALF, length), np.float64)
    for inner in range(length):
        result[inner : inner + TAPS, inner] = weights
    return result


def two(matrix):
    high = np.asarray(matrix, np.float32).astype(BF16)
    low = (matrix - high.astype(np.float64)).astype(np.float32).astype(BF16)
    return high, low


def row_weights(height):
    return np.concatenate([part.T for part in two(band(height))], axis=0)


def column_weights(width):
    matrix = band(width)
    left, own, right = matrix[:HALF], matrix[HALF : HALF + width], matrix[HALF + width :]
    result = []
    for h in range(2):
        for q in range(4):
            halo = np.zeros((width, width))
            first, second = (left, right) if h == 0 else (right, left)
            halo[32 * q : 32 * q + HALF] = first
            halo[32 * q + HALF : 32 * q + 2 * HALF] = second
            result.append(np.concatenate(two(np.concatenate([own, halo], axis=0)), axis=1))
    return np.stack(result)


def strip_selector(width):
    result = np.zeros((8, width, 2 * width), np.float32)
    for h in range(2):
        for q in range(4):
            for c in range(HALF):
                result[4 * h + q, width - HALF + c, 32 * q + HALF * h + c] = 1
                result[4 * h + q, c, width + 32 * q + HALF * (1 - h) + c] = 1
    return result.reshape(8 * width, 2 * width).astype(BF16)


def dot(a, b):
    return jnp.dot(a, b, preferred_element_type=F32)


def split(value):
    high = value.astype(BF16)
    return high, (value - high.astype(F32)).astype(BF16)


def strips_kernel(top, own, bottom, select, last, first):
    width = own.shape[3]
    for g in range(8):
        parts = [jnp.concatenate([top[g, k], own[g, k], bottom[g, k]], axis=0) for k in range(8)]
        both = dot(jnp.concatenate(parts, axis=1), select[...]).astype(BF16)
        last[g] = both[:, :width]
        first[g] = both[:, width:]


def rows_kernel(top, own, bottom, weights, high, low):
    height, width = own.shape[2:]
    for g in range(8):
        for k in range(0, 8, 2):
            parts = [jnp.concatenate([top[g, i], own[g, i], bottom[g, i]], axis=0) for i in (k, k + 1)]
            both = dot(weights[...], jnp.concatenate(parts, axis=1))
            upper, lower = split(both[:height] + both[height:])
            high[g, k], high[g, k + 1] = upper[:, :width], upper[:, width:]
            low[g, k], low[g, k + 1] = lower[:, :width], lower[:, width:]


def columns_kernel(points, high, low, left, right, weights, across, field, packed, halo_high, halo_low, flat):
    height, width = high.shape[2:]
    lane = lax.broadcasted_iota(jnp.int32, left.shape[1:], 1)
    even = (lane // HALF) % 2 == 0
    for g in range(8):
        a, b = left[g].astype(F32), right[g].astype(F32)
        both = jnp.concatenate([jnp.where(even, a, b), jnp.where(even, b, a)], axis=1).astype(BF16)
        both = dot(weights[...], both)
        upper, lower = split(both[:height] + both[height:])
        halo_high[g], halo_low[g] = upper, lower
    for k in range(8):
        lanes = slice(width * (k // 4), width * (k // 4 + 1))
        for g in range(8):
            upper = jnp.concatenate([high[g, k], halo_high[g, :, lanes]], axis=1)
            lower = jnp.concatenate([low[g, k], halo_low[g, :, lanes]], axis=1)
            both = dot(upper, across[k])
            value = both[:, :width] + both[:, width:] + dot(lower, across[k, :, :width])
            flat[pl.ds((8 * g + k) * height, height), :] = value
    count = 64
    for r in range(height):
        upper, lower = split(flat[pl.ds(r, count, stride=height), :])
        field[:count, r * width : (r + 1) * width] = upper
        field[count:, r * width : (r + 1) * width] = lower
    total = jnp.zeros((2 * count, 2 * count), F32)
    size = 2048
    for start in range(0, height * width, size):
        part = field[:, start : start + size]
        total = total + lax.dot_general(part, part, (((1,), (1,)), ((), ())), preferred_element_type=F32)
    gram = total[:count, :count] + total[count:, count:] + (total[:count, count:] + total[count:, :count])
    packed[...] = gram / points


def factor(gram, size=8):
    count = gram.shape[0]
    row = lax.broadcasted_iota(jnp.int32, gram.shape, 0)
    col = lax.broadcasted_iota(jnp.int32, gram.shape, 1)
    a = jnp.concatenate([gram, jnp.where(row == col, 1.0, 0.0).astype(F32)], axis=1)
    rows = []
    for k in range(0, count, size):
        columns = [jnp.broadcast_to(a[:, k + i : k + i + 1], a.shape) for i in range(size)]
        lower, scale = {}, []
        for j in range(size):
            pivot = columns[j][k + j : k + j + 1]
            for m in range(j):
                pivot = pivot - lower[j, m] * lower[j, m]
            scale.append(lax.rsqrt(pivot))
            for i in range(j + 1, size):
                entry = columns[j][k + i : k + i + 1]
                for m in range(j):
                    entry = entry - lower[i, m] * lower[j, m]
                lower[i, j] = entry * scale[j]

        def solve(values):
            done = []
            for i in range(size):
                value = values[i]
                for m in range(i):
                    value = value - lower[i, m] * done[m]
                done.append(value * scale[i])
            return done

        new = solve([a[k + i : k + i + 1] for i in range(size)])
        rows += new
        if k + size < count:
            multipliers = solve(columns)
            for m in range(size):
                a = a - multipliers[m] * new[m]
    return rows


def basis_kernel(gram, field, basis, upper, work, inverse):
    count = gram.shape[0]

    @pl.when(pl.program_id(0) == 0)
    def _():
        for k, value in enumerate(factor(gram[...])):
            work[k : k + 1, :] = value
        row = lax.broadcasted_iota(jnp.int32, (count, count), 0)
        col = lax.broadcasted_iota(jnp.int32, (count, count), 1)
        both = work[...]
        upper[...] = jnp.where(row <= col, both[:, :count], 0.0)
        high, low = split(jnp.where(row >= col, both[:, count:], 0.0))
        top = jnp.concatenate([high, high], axis=1)
        bottom = jnp.concatenate([low, jnp.zeros_like(low)], axis=1)
        inverse[...] = jnp.concatenate([top, bottom], axis=0)

    width = basis.shape[2]
    both = dot(inverse[...], field[...])
    value = both[:count] + both[count:]
    for r in range(basis.shape[1]):
        basis[:, r, :] = value[:, r * width : (r + 1) * width]


def whole(n):
    return [pl.BlockSpec(memory_space=pltpu.VMEM)] * n


def shape(*dims, dtype=BF16):
    return jax.ShapeDtypeStruct(dims, dtype)


def strips(top, own, bottom):
    height, width = own.shape[1] + 2 * HALF, own.shape[2]
    args = [v.reshape(8, 8, *v.shape[1:]) for v in (top, own, bottom)]
    return pl.pallas_call(
        strips_kernel,
        out_shape=[shape(8, height, width)] * 2,
        in_specs=whole(4),
        out_specs=whole(2),
        compiler_params=pltpu.CompilerParams(vmem_limit_bytes=16 << 20),
    )(*args, jnp.asarray(strip_selector(width)))


def filter_rows(top, own, bottom):
    height, width = own.shape[1:]
    args = [v.reshape(8, 8, *v.shape[1:]) for v in (top, own, bottom)]
    return pl.pallas_call(
        rows_kernel,
        out_shape=[shape(8, 8, height, width)] * 2,
        in_specs=whole(4),
        out_specs=whole(2),
        compiler_params=pltpu.CompilerParams(vmem_limit_bytes=16 << 20),
        cost_estimate=pl.CostEstimate(
            flops=4 * own.size * (height + 2 * HALF), bytes_accessed=6 * own.size, transcendentals=0
        ),
    )(*args, jnp.asarray(row_weights(height)))


def filter_columns(high, low, left, right, points):
    height, width = high.shape[2:]
    return pl.pallas_call(
        functools.partial(columns_kernel, points),
        out_shape=[shape(128, height * width), shape(64, 64, dtype=F32)],
        in_specs=whole(6),
        out_specs=whole(2),
        compiler_params=pltpu.CompilerParams(vmem_limit_bytes=24 << 20),
        scratch_shapes=[pltpu.VMEM((8, height, 2 * width), BF16)] * 2 + [pltpu.VMEM((64 * height, width), F32)],
    )(high, low, left, right, jnp.asarray(row_weights(height)), jnp.asarray(column_weights(width)))


def orthonormal(gram, field, height, width):
    count = gram.shape[0]
    return pl.pallas_call(
        basis_kernel,
        grid=(height // STEP,),
        compiler_params=pltpu.CompilerParams(vmem_limit_bytes=24 << 20),
        out_shape=[shape(count, height, width, dtype=F32), shape(count, count, dtype=F32)],
        in_specs=[pl.BlockSpec((count, count), lambda i: (0, 0)), pl.BlockSpec((2 * count, STEP * width), lambda i: (0, i))],
        out_specs=[pl.BlockSpec((count, STEP, width), lambda i: (0, i, 0)), pl.BlockSpec((count, count), lambda i: (0, 0))],
        scratch_shapes=[pltpu.VMEM((count, 2 * count), F32), pltpu.VMEM((2 * count, 2 * count), BF16)],
    )(gram, field)


def pack(gram):
    half = gram.shape[0] // 2
    first, second = gram[:half, :half], gram[half:, half:]
    row = lax.broadcasted_iota(jnp.int32, (half, half), 0)
    col = lax.broadcasted_iota(jnp.int32, (half, half), 1)
    mixed = jnp.where(row >= col, first, second)
    diagonal = jnp.sum(jnp.where(row == col, second, 0.0), axis=0)
    diagonal = jnp.pad(diagonal, (0, half))[None]
    top = jnp.concatenate([gram[half:, :half], mixed], axis=1)
    return jnp.concatenate([top, diagonal, jnp.zeros_like(diagonal)], axis=0)


def unpack(packed):
    half = packed.shape[1] // 2
    cross, mixed, diagonal = packed[:half, :half], packed[:half, half:], packed[half, :half]
    row = lax.broadcasted_iota(jnp.int32, (half, half), 0)
    col = lax.broadcasted_iota(jnp.int32, (half, half), 1)
    first = jnp.where(row >= col, mixed, mixed.T)
    second = jnp.where(row < col, mixed, mixed.T)
    second = jnp.where(row == col, diagonal[None], second)
    return jnp.concatenate(
        [jnp.concatenate([first, cross.T], axis=1), jnp.concatenate([cross, second], axis=1)], axis=0
    )


def summed(array, axis):
    copies = jnp.broadcast_to(array[None], (lax.axis_size(axis),) + array.shape)
    return lax.all_to_all(copies, axis, 0, 0).sum(0)


def swap(upward, downward, axis):
    devices = lax.axis_size(axis)
    up = [(i, (i + 1) % devices) for i in range(devices)]
    down = [(j, i) for i, j in up]
    return lax.ppermute(upward, axis, up), lax.ppermute(downward, axis, down)


def local(snapshots):
    count, height, width = snapshots.shape
    points = height * width * lax.axis_size("row") * lax.axis_size("col")
    top, bottom = swap(snapshots[:, height - HALF :], snapshots[:, :HALF], "row")
    left, right = swap(*strips(top, snapshots, bottom), "col")
    high, low = filter_rows(top, snapshots, bottom)
    field, gram = filter_columns(high, low, left, right, points)
    total = pack(gram).reshape(-1)
    total = summed(summed(total, "row"), "col")
    gram = unpack(total.reshape(count // 2 + 2, count))
    return tuple(orthonormal(gram, field, height, width))


def solution(mesh):
    return jax.shard_map(
        local,
        mesh=mesh,
        in_specs=(P(None, "row", "col"),),
        out_specs=(P(None, "row", "col"), P()),
        check_vma=False,
    )
```

time: 106 us -> 82.7 us (0.78)
  matrix products: 17.6 us -> 0 us
  other arithmetic: 15.1 us -> 0.59 us
  Pallas kernels: 0 us -> 13.1 us
  local copies, waits for them, and re-layouts: 12.5 us -> 4.23 us
  starting transfers between devices: 18.4 us -> 21.8 us
  waiting for transfers between devices: 3.15 us -> 6.16 us
  blocking collectives: 37.9 us -> 35.8 us
    dot_general x4 -> x0, matrix products: 17.4 us -> none  [the longest x1 6.69 us: filter_columns(): jnp.einsum('src,cd->srd', field, band_matrix(width), precision=lax.Precis...]
    pallas_call x0 -> x4, Pallas kernels: none -> 13.1 us  [the longest x1 5.85 us: filter_columns(): pl.pallas_call(functools.partial(columns_kernel, points), out_shape=[shap...]
    another operation x4 -> x0, other arithmetic: 11.4 us -> none  [the longest x3 6.53 us: local(): upper = jnp.linalg.cholesky(gram, symmetrize_input=False).T]
    unnamed x8 -> x11, local copies, waits for them, and re-layouts: 7.37 us -> 2.54 us
    ppermute x2 -> x0, local copies, waits for them, and re-layouts: 3.49 us -> none  [the longest x1 1.78 us: padded(): before = lax.ppermute(last, axis, up)]
    ppermute x4, starting transfers between devices: 18.4 us -> 21.8 us  [swap(): return (lax.ppermute(upward, axis, up), lax.ppermute(downward, axis, down))]
    ppermute x4, waiting for transfers between devices: 3.15 us -> 6.16 us  [swap(): return (lax.ppermute(upward, axis, up), lax.ppermute(downward, axis, down))]
    all_to_all x2, blocking collectives: 37.9 us -> 35.8 us  [summed(): return lax.all_to_all(copies, axis, 0, 0).sum(0)]
  transfers between devices with their start and end apart: 4 -> 4, of which waited for: 2 -> 4; matrix products, arithmetic and copies ran while one was open for 5% -> 0% of each run, Pallas kernels for 0% -> 1%
where the time goes in v2:
time: 82.7 us; the launch traced here: 82.4 us
  blocking collectives  35.8 us (43%)
  starting transfers between devices  21.8 us (26%)
  Pallas kernels  13.1 us (16%)
  waiting for transfers between devices  6.16 us (7%)
  local copies, waits for them, and re-layouts  4.23 us (5%)
    all_to_all x2, blocking collectives, summed(): return lax.all_to_all(copies, axis, 0, 0).sum(0)  35.8 us
    ppermute x4, starting transfers between devices, swap(): return (lax.ppermute(upward, axis, up), lax.ppermute(downward, axis, down))  21.8 us
    ppermute x4, waiting for transfers between devices, swap(): return (lax.ppermute(upward, axis, up), lax.ppermute(downward, axis, down))  6.16 us
    pallas_call x1, Pallas kernels, filter_columns(): pl.pallas_call(functools.partial(columns_kernel, points), out_shape=[shap...  5.85 us
    pallas_call x1, Pallas kernels, orthonormal(): pl.pallas_call(basis_kernel, grid=(height // STEP,), compiler_params=pltp...  5.56 us
    unnamed x11, local copies, waits for them, and re-layouts  2.54 us
  transfers between devices with their start and end apart: 4, of which 4 were waited for; matrix products, arithmetic and copies ran while one was open for 0% of the time, Pallas kernels for 1%

profile of v2, /device:TPU:1, one launch (start us, length us, event | category | flops | bytes accessed | tf_op | source)
XLA Modules:
  0.0 82.4 jit_solution(6965229840619718744)
XLA Ops:
  0.6 0.0 copy-start.4
  0.6 1.1 %fusion.1 = (bf16[64,16,128]{2,1,0:T(8,128)(2,1)S(1)}, bf16[64,16,128]{2,1,0:T(8,128)(2,1)S(1)}) fusion(bf16[64,96,128]{2,1,0:T(8,128)(2,1)} %param.5), kind=kLoop, calls=%fused_computation.12 | loop fusion | bytes 1048576 | tf_op jit(solution)/shard_map/slice | solution.py:283
  1.7 2.7 %collective-permute-start = (bf16[64,16,128]{2,1,0:T(8,128)(2,1)S(1)}, bf16[64,16,128]{2,1,0:T(8,128)(2,1)S(1)}, u32[]{:S(2)}, u32[]{:S(2)}) collective-permute-start(bf16[64,16,128]{2,1,0:T(8,128)(2,1)S(1)} %get-tuple-element.15), channel_id=1, source_target_pairs={{0,32},{32,64},{64,96},{96,128},{128,160},{160,192},{192,224},{224... | collective-permute-start | bytes 786440 | tf_op jit(solution)/shard_map/ppermute | solution.py:277
  4.4 4.2 %collective-permute-start.1 = (bf16[64,16,128]{2,1,0:T(8,128)(2,1)S(1)}, bf16[64,16,128]{2,1,0:T(8,128)(2,1)S(1)}, u32[]{:S(2)}, u32[]{:S(2)}) collective-permute-start(bf16[64,16,128]{2,1,0:T(8,128)(2,1)S(1)} %get-tuple-element.14), channel_id=1, source_target_pairs={{32,0},{64,32},{96,64},{128,96},{160,128},{192,160},{224,192},{256... | collective-permute-start | bytes 786440 | tf_op jit(solution)/shard_map/ppermute | solution.py:277
  8.6 1.0 %collective-permute-done = bf16[64,16,128]{2,1,0:T(8,128)(2,1)S(1)} collective-permute-done((bf16[64,16,128]{2,1,0:T(8,128)(2,1)S(1)}, bf16[64,16,128]{2,1,0:T(8,128)(2,1)S(1)}, u32[]{:S(2)}, u32[]{:S(2)}) %collective-permute-start) | collective-permute-done | bytes 262176 | tf_op jit(solution)/shard_map/ppermute | solution.py:277
  9.6 0.6 collective-permute-done.1
  10.2 0.0 copy-start
  10.2 1.4 %copy-done = bf16[64,96,128]{2,1,0:T(8,128)(2,1)S(1)} copy-done((bf16[64,96,128]{2,1,0:T(8,128)(2,1)S(1)}, bf16[64,96,128]{2,1,0:T(8,128)(2,1)}, u32[]{:S(2)}) %copy-start) | copy-done | bytes 1572888
  11.6 0.0 copy-start.3
  11.6 1.0 %copy-done.3 = bf16[1024,256]{1,0:T(8,128)(2,1)S(1)} copy-done((bf16[1024,256]{1,0:T(8,128)(2,1)S(1)}, bf16[1024,256]{1,0:T(8,128)(2,1)}, u32[]{:S(2)}) %copy-start.3) | copy-done | bytes 524312
  12.7 0.0 copy-start.1
  12.7 0.7 shard_map.69
  13.4 0.0 copy-start.2
  13.4 3.2 %collective-permute-start.2 = (bf16[8,128,128]{2,1,0:T(8,128)(2,1)S(1)}, bf16[8,128,128]{2,1,0:T(8,128)(2,1)S(1)}, u32[]{:S(2)}, u32[]{:S(2)}) collective-permute-start(bf16[8,128,128]{2,1,0:T(8,128)(2,1)S(1)} %get-tuple-element.10), channel_id=1, source_target_pairs={{0,1},{1,2},{2,3},{3,4},{4,5},{5,6},{6,7},{7,8},{8,9},{9,10},{10,1... | collective-permute-start | bytes 786440 | tf_op jit(solution)/shard_map/ppermute | solution.py:277
  16.7 11.7 %collective-permute-start.3 = (bf16[8,128,128]{2,1,0:T(8,128)(2,1)S(1)}, bf16[8,128,128]{2,1,0:T(8,128)(2,1)S(1)}, u32[]{:S(2)}, u32[]{:S(2)}) collective-permute-start(bf16[8,128,128]{2,1,0:T(8,128)(2,1)S(1)} %get-tuple-element.11), channel_id=1, source_target_pairs={{1,0},{2,1},{3,2},{4,3},{5,4},{6,5},{7,6},{8,7},{9,8},{10,9},{11,1... | collective-permute-start | bytes 786440 | tf_op jit(solution)/shard_map/ppermute | solution.py:277
  28.3 0.1 pad.12.clone
  28.4 0.0 copy-done.4
  28.4 0.0 copy-done.1
  28.4 1.0 %shard_map.68 = (bf16[8,8,96,128]{3,2,1,0:T(8,128)(2,1)S(1)}, bf16[8,8,96,128]{3,2,1,0:T(8,128)(2,1)S(1)}) custom-call(bf16[8,8,16,128]{3,2,1,0:T(8,128)(2,1)S(1)} %bitcast.17, bf16[8,8,96,128]{3,2,1,0:T(8,128)(2,1)S(1)} %bitcast.15, bf16[8,8,16,128]{3,2,1,0:T(8,128)(2,1)S(1)} %bitcast.19, bf16[192,128]{1,0:T(8,128)(2,1)S(1)} %copy-done.4), custom_call_target="tpu_custom_call" | custom-call | flops 402653184 | bytes 4718592 | tf_op jit(solution)/shard_map/pallas_call | solution.py:206
  29.4 3.6 %collective-permute-done.2.left = bf16[8,128,128]{2,1,0:T(8,128)(2,1)S(1)} collective-permute-done((bf16[8,128,128]{2,1,0:T(8,128)(2,1)S(1)}, bf16[8,128,128]{2,1,0:T(8,128)(2,1)S(1)}, u32[]{:S(2)}, u32[]{:S(2)}) %collective-permute-start.2) | collective-permute-done | bytes 262176 | tf_op jit(solution)/shard_map/ppermute | solution.py:277
  33.0 0.9 %collective-permute-done.3.right = bf16[8,128,128]{2,1,0:T(8,128)(2,1)S(1)} collective-permute-done((bf16[8,128,128]{2,1,0:T(8,128)(2,1)S(1)}, bf16[8,128,128]{2,1,0:T(8,128)(2,1)S(1)}, u32[]{:S(2)}, u32[]{:S(2)}) %collective-permute-start.3) | collective-permute-done | bytes 262176 | tf_op jit(solution)/shard_map/ppermute | solution.py:277
  34.0 0.0 copy-done.2
  34.0 5.8 %shard_map.70 = (bf16[128,12288]{1,0:T(8,128)(2,1)S(1)}, f32[64,64]{1,0:T(8,128)S(1)}) custom-call(bf16[8,8,96,128]{3,2,1,0:T(8,128)(2,1)S(1)} %get-tuple-element.8.high, bf16[8,8,96,128]{3,2,1,0:T(8,128)(2,1)S(1)} %get-tuple-element.9.low, bf16[8,128,128]{2,1,0:T(8,128)(2,1)S(1)} %collective-permute-done.2.left, ...), custom_call_target="tpu_custom_call" | custom-call | tf_op jit(solution)/shard_map/pallas_call | solution.py:220
  39.8 0.1 fusion.2
  39.9 0.1 maximum_maximum_fusion.1
  40.0 0.1 broadcast_in_dim.36
  40.1 0.1 broadcast_in_dim.37
  40.1 16.3 %all_to_all.12 = f32[16,1,2176]{2,1,0:T(1,128)S(1)} all-to-all(f32[16,1,2176]{2,1,0:T(1,128)S(1)} %broadcast_in_dim.37), channel_id=1, replica_groups=mesh['row'=16,'col'=32] {'row'}, dimensions={0} | all-to-all | bytes 278528 | tf_op jit(solution)/shard_map/all_to_all | solution.py:270
  56.4 0.1 reduce_sum.28
  56.5 0.1 broadcast_in_dim.38
  56.7 19.6 %all_to_all.13 = f32[32,1,2176]{2,1,0:T(1,128)S(1)} all-to-all(f32[32,1,2176]{2,1,0:T(1,128)S(1)} %broadcast_in_dim.38), channel_id=1, replica_groups=mesh['row'=16,'col'=32] {'col'}, dimensions={0} | all-to-all | bytes 557056 | tf_op jit(solution)/shard_map/all_to_all | solution.py:270
  76.2 0.2 reduce_sum.29
  76.4 0.1 reshape.36
  76.5 0.1 slice.32
  76.5 0.1 copy.18
  76.6 0.1 bitcast_select_fusion.1
  76.7 0.1 copy.23
  76.8 0.1 maximum_maximum_fusion.gram
  76.8 5.6 %shard_map.71 = (f32[64,96,128]{2,1,0:T(8,128)}, f32[64,64]{1,0:T(8,128)}) custom-call(f32[64,64]{1,0:T(8,128)S(1)} %maximum_maximum_fusion.gram, bf16[128,12288]{1,0:T(8,128)(2,1)S(1)} %get-tuple-element.13.field), custom_call_target="tpu_custom_call" | custom-call | tf_op jit(solution)/shard_map/pallas_call | solution.py:232
  (2 shorter events, 0.0 us)
Async XLA Ops:
  0.6 27.8 %copy-start.4 = (bf16[192,128]{1,0:T(8,128)(2,1)S(1)}, bf16[192,128]{1,0:T(8,128)(2,1)}, u32[]{:S(2)}) copy-start(bf16[192,128]{1,0:T(8,128)(2,1)} %constant.12.clone.weights) | copy-start | bytes 147460
  1.7 7.9 %collective-permute-start = (bf16[64,16,128]{2,1,0:T(8,128)(2,1)S(1)}, bf16[64,16,128]{2,1,0:T(8,128)(2,1)S(1)}, u32[]{:S(2)}, u32[]{:S(2)}) collective-permute-start(bf16[64,16,128]{2,1,0:T(8,128)(2,1)S(1)} %get-tuple-element.15), channel_id=1, source_target_pairs={{0,32},{32,64},{64,96},{96,128},{128,160},{160,192},{192,224},{224... | collective-permute-start | bytes 786440 | tf_op jit(solution)/shard_map/ppermute | solution.py:277
  4.4 5.8 %collective-permute-start.1 = (bf16[64,16,128]{2,1,0:T(8,128)(2,1)S(1)}, bf16[64,16,128]{2,1,0:T(8,128)(2,1)S(1)}, u32[]{:S(2)}, u32[]{:S(2)}) collective-permute-start(bf16[64,16,128]{2,1,0:T(8,128)(2,1)S(1)} %get-tuple-element.14), channel_id=1, source_target_pairs={{32,0},{64,32},{96,64},{128,96},{160,128},{192,160},{224,192},{256... | collective-permute-start | bytes 786440 | tf_op jit(solution)/shard_map/ppermute | solution.py:277
  10.2 1.4 %copy-start = (bf16[64,96,128]{2,1,0:T(8,128)(2,1)S(1)}, bf16[64,96,128]{2,1,0:T(8,128)(2,1)}, u32[]{:S(2)}) copy-start(bf16[64,96,128]{2,1,0:T(8,128)(2,1)} %param.5) | copy-start | bytes 4718596
  11.6 1.0 %copy-start.3 = (bf16[1024,256]{1,0:T(8,128)(2,1)S(1)}, bf16[1024,256]{1,0:T(8,128)(2,1)}, u32[]{:S(2)}) copy-start(bf16[1024,256]{1,0:T(8,128)(2,1)} %constant.5.clone.select) | copy-start | bytes 1572868
  12.7 15.8 %copy-start.1 = (bf16[64,96,128]{2,1,0:T(8,128)(2,1)S(1)}, bf16[64,96,128]{2,1,0:T(8,128)(2,1)}, u32[]{:S(2)}) copy-start(bf16[64,96,128]{2,1,0:T(8,128)(2,1)} %param.5) | copy-start | bytes 4718596
  13.4 20.6 %copy-start.2 = (bf16[8,256,256]{2,1,0:T(8,128)(2,1)S(1)}, bf16[8,256,256]{2,1,0:T(8,128)(2,1)}, u32[]{:S(2)}) copy-start(bf16[8,256,256]{2,1,0:T(8,128)(2,1)} %constant.13.clone.across) | copy-start | bytes 3145732
  13.4 19.6 %collective-permute-start.2 = (bf16[8,128,128]{2,1,0:T(8,128)(2,1)S(1)}, bf16[8,128,128]{2,1,0:T(8,128)(2,1)S(1)}, u32[]{:S(2)}, u32[]{:S(2)}) collective-permute-start(bf16[8,128,128]{2,1,0:T(8,128)(2,1)S(1)} %get-tuple-element.10), channel_id=1, source_target_pairs={{0,1},{1,2},{2,3},{3,4},{4,5},{5,6},{6,7},{7,8},{8,9},{9,10},{10,1... | collective-permute-start | bytes 786440 | tf_op jit(solution)/shard_map/ppermute | solution.py:277
  16.7 17.3 %collective-permute-start.3 = (bf16[8,128,128]{2,1,0:T(8,128)(2,1)S(1)}, bf16[8,128,128]{2,1,0:T(8,128)(2,1)S(1)}, u32[]{:S(2)}, u32[]{:S(2)}) collective-permute-start(bf16[8,128,128]{2,1,0:T(8,128)(2,1)S(1)} %get-tuple-element.11), channel_id=1, source_target_pairs={{1,0},{2,1},{3,2},{4,3},{5,4},{6,5},{7,6},{8,7},{9,8},{10,9},{11,1... | collective-permute-start | bytes 786440 | tf_op jit(solution)/shard_map/ppermute | solution.py:277

commit v3 on v2

--- a/solution.py
+++ b/solution.py
@@ -48,16 +48,6 @@
     return np.stack(result)
 
 
-def strip_selector(width):
-    result = np.zeros((8, width, 2 * width), np.float32)
-    for h in range(2):
-        for q in range(4):
-            for c in range(HALF):
-                result[4 * h + q, width - HALF + c, 32 * q + HALF * h + c] = 1
-                result[4 * h + q, c, width + 32 * q + HALF * (1 - h) + c] = 1
-    return result.reshape(8 * width, 2 * width).astype(BF16)
-
-
 def dot(a, b):
     return jnp.dot(a, b, preferred_element_type=F32)
 
@@ -67,13 +57,28 @@
     return high, (value - high.astype(F32)).astype(BF16)
 
 
-def strips_kernel(top, own, bottom, select, last, first):
-    width = own.shape[3]
+def selector(width):
+    row = lax.broadcasted_iota(jnp.int32, (width, width), 0)
+    shift = lax.broadcasted_iota(jnp.int32, (width, width), 1) - row
+    blocks = []
+    for k in range(8):
+        h, q = k // 4, k % 4
+        last = (shift == 32 * q + HALF * h + HALF - width) & (row >= width - HALF)
+        first = (shift == 32 * q + HALF * (1 - h)) & (row < HALF)
+        both = [jnp.where(mask, 1.0, 0.0).astype(BF16) for mask in (last, first)]
+        blocks.append(jnp.concatenate(both, axis=1))
+    return jnp.concatenate(blocks, axis=0)
+
+
+def edges_kernel(own, last_columns, first_columns, last_rows, first_rows):
+    height, width = own.shape[2:]
+    parts = [jnp.concatenate([own[g, k] for k in range(8)], axis=1) for g in range(8)]
+    both = dot(jnp.concatenate(parts, axis=0), selector(width)).astype(BF16)
     for g in range(8):
-        parts = [jnp.concatenate([top[g, k], own[g, k], bottom[g, k]], axis=0) for k in range(8)]
-        both = dot(jnp.concatenate(parts, axis=1), select[...]).astype(BF16)
-        last[g] = both[:, :width]
-        first[g] = both[:, width:]
+        last_columns[g] = both[g * height : (g + 1) * height, :width]
+        first_columns[g] = both[g * height : (g + 1) * height, width:]
+    last_rows[...] = own[:, :, height - HALF :, :]
+    first_rows[...] = own[:, :, :HALF, :]
 
 
 def rows_kernel(top, own, bottom, weights, high, low):
@@ -87,12 +92,15 @@
             low[g, k], low[g, k + 1] = lower[:, :width], lower[:, width:]
 
 
-def columns_kernel(points, high, low, left, right, weights, across, field, packed, halo_high, halo_low, flat):
+def columns_kernel(points, high, low, left, right, top, bottom, weights, across, field, packed, halo_high, halo_low, flat):
     height, width = high.shape[2:]
-    lane = lax.broadcasted_iota(jnp.int32, left.shape[1:], 1)
+    lane = lax.broadcasted_iota(jnp.int32, (height + 2 * HALF, width), 1)
     even = (lane // HALF) % 2 == 0
     for g in range(8):
-        a, b = left[g].astype(F32), right[g].astype(F32)
+        a, b = [
+            jnp.concatenate([top[i], side[g], bottom[i]], axis=0).astype(F32)
+            for side, i in ((left, g), (right, 8 + g))
+        ]
         both = jnp.concatenate([jnp.where(even, a, b), jnp.where(even, b, a)], axis=1).astype(BF16)
         both = dot(weights[...], both)
         upper, lower = split(both[:height] + both[height:])
@@ -104,10 +112,10 @@
             lower = jnp.concatenate([low[g, k], halo_low[g, :, lanes]], axis=1)
             both = dot(upper, across[k])
             value = both[:, :width] + both[:, width:] + dot(lower, across[k, :, :width])
-            flat[pl.ds((8 * g + k) * height, height), :] = value
+            flat[pl.ds((8 * g + k) * (height + 8), height), :] = value
     count = 64
     for r in range(height):
-        upper, lower = split(flat[pl.ds(r, count, stride=height), :])
+        upper, lower = split(flat[pl.ds(r, count, stride=height + 8), :])
         field[:count, r * width : (r + 1) * width] = upper
         field[count:, r * width : (r + 1) * width] = lower
     total = jnp.zeros((2 * count, 2 * count), F32)
@@ -188,21 +196,22 @@
     return jax.ShapeDtypeStruct(dims, dtype)
 
 
-def strips(top, own, bottom):
-    height, width = own.shape[1] + 2 * HALF, own.shape[2]
-    args = [v.reshape(8, 8, *v.shape[1:]) for v in (top, own, bottom)]
+def edges(own):
+    height, width = own.shape[2:]
     return pl.pallas_call(
-        strips_kernel,
-        out_shape=[shape(8, height, width)] * 2,
-        in_specs=whole(4),
-        out_specs=whole(2),
+        edges_kernel,
+        out_shape=[shape(8, height, width)] * 2 + [shape(8, 8, HALF, width)] * 2,
+        in_specs=whole(1),
+        out_specs=whole(4),
         compiler_params=pltpu.CompilerParams(vmem_limit_bytes=16 << 20),
-    )(*args, jnp.asarray(strip_selector(width)))
+        cost_estimate=pl.CostEstimate(
+            flops=4 * width * own.size, bytes_accessed=3 * own.size, transcendentals=0
+        ),
+    )(own)
 
 
 def filter_rows(top, own, bottom):
-    height, width = own.shape[1:]
-    args = [v.reshape(8, 8, *v.shape[1:]) for v in (top, own, bottom)]
+    height, width = own.shape[2:]
     return pl.pallas_call(
         rows_kernel,
         out_shape=[shape(8, 8, height, width)] * 2,
@@ -212,19 +221,19 @@
         cost_estimate=pl.CostEstimate(
             flops=4 * own.size * (height + 2 * HALF), bytes_accessed=6 * own.size, transcendentals=0
         ),
-    )(*args, jnp.asarray(row_weights(height)))
-
-
-def filter_columns(high, low, left, right, points):
+    )(top, own, bottom, jnp.asarray(row_weights(height)))
+
+
+def filter_columns(high, low, sides, points):
     height, width = high.shape[2:]
     return pl.pallas_call(
         functools.partial(columns_kernel, points),
         out_shape=[shape(128, height * width), shape(64, 64, dtype=F32)],
-        in_specs=whole(6),
+        in_specs=whole(8),
         out_specs=whole(2),
         compiler_params=pltpu.CompilerParams(vmem_limit_bytes=24 << 20),
-        scratch_shapes=[pltpu.VMEM((8, height, 2 * width), BF16)] * 2 + [pltpu.VMEM((64 * height, width), F32)],
-    )(high, low, left, right, jnp.asarray(row_weights(height)), jnp.asarray(column_weights(width)))
+        scratch_shapes=[pltpu.VMEM((8, height, 2 * width), BF16)] * 2 + [pltpu.VMEM((64 * (height + 8), width), F32)],
+    )(high, low, *sides, jnp.asarray(row_weights(height)), jnp.asarray(column_weights(width)))
 
 
 def orthonormal(gram, field, height, width):
@@ -280,10 +289,16 @@
 def local(snapshots):
     count, height, width = snapshots.shape
     points = height * width * lax.axis_size("row") * lax.axis_size("col")
-    top, bottom = swap(snapshots[:, height - HALF :], snapshots[:, :HALF], "row")
-    left, right = swap(*strips(top, snapshots, bottom), "col")
-    high, low = filter_rows(top, snapshots, bottom)
-    field, gram = filter_columns(high, low, left, right, points)
+    own = snapshots.reshape(8, 8, height, width)
+    last_columns, first_columns, last_rows, first_rows = edges(own)
+    sides = swap(last_columns, first_columns, "col")
+    top, bottom = swap(last_rows, first_rows, "row")
+    last_rows, first_rows = [
+        jnp.concatenate([side[:, rows] for side in sides], axis=0) for rows in (slice(height - HALF, None), slice(HALF))
+    ]
+    corners = swap(last_rows, first_rows, "row")
+    high, low = filter_rows(top, own, bottom)
+    field, gram = filter_columns(high, low, (*sides, *corners), points)
     total = pack(gram).reshape(-1)
     total = summed(summed(total, "row"), "col")
     gram = unpack(total.reshape(count // 2 + 2, count))

time: 82.7 us -> 76.4 us (0.924)
  waiting for transfers between devices: 6.16 us -> 4.02 us
  local copies, waits for them, and re-layouts: 4.23 us -> 2.1 us
  starting transfers between devices: 21.8 us -> 20.6 us
  Pallas kernels: 13.1 us -> 12.2 us
    ppermute x4 -> x6, waiting for transfers between devices: 6.16 us -> 4.02 us  [swap(): return (lax.ppermute(upward, axis, up), lax.ppermute(downward, axis, down))]
    ppermute x4 -> x6, starting transfers between devices: 21.8 us -> 20.6 us  [swap(): return (lax.ppermute(upward, axis, up), lax.ppermute(downward, axis, down))]
    slice x1 -> x2, local copies, waits for them, and re-layouts: 1.09 us -> 0.01 us  [local(): side[:, rows]]
    unnamed x11 -> x7, local copies, waits for them, and re-layouts: 2.54 us -> 1.48 us
  transfers between devices with their start and end apart: 4 -> 6, of which waited for: 4 -> 4; matrix products, arithmetic and copies ran while one was open for 0% -> 0% of each run, Pallas kernels for 1% -> 1%
where the time goes in v3:
time: 76.4 us; the launch traced here: 76.2 us
  blocking collectives  35.8 us (47%)
  starting transfers between devices  20.6 us (27%)
  Pallas kernels  12.2 us (16%)
  waiting for transfers between devices  4.02 us (5%)
  local copies, waits for them, and re-layouts  2.1 us (3%)
    all_to_all x2, blocking collectives, summed(): return lax.all_to_all(copies, axis, 0, 0).sum(0)  35.8 us
    ppermute x6, starting transfers between devices, swap(): return (lax.ppermute(upward, axis, up), lax.ppermute(downward, axis, down))  20.6 us
    pallas_call x1, Pallas kernels, orthonormal(): pl.pallas_call(basis_kernel, grid=(height // STEP,), compiler_params=pltp...  5.56 us
    pallas_call x1, Pallas kernels, filter_columns(): pl.pallas_call(functools.partial(columns_kernel, points), out_shape=[shap...  5.14 us
    ppermute x6, waiting for transfers between devices, swap(): return (lax.ppermute(upward, axis, up), lax.ppermute(downward, axis, down))  4.02 us
  transfers between devices with their start and end apart: 6, of which 4 were waited for; matrix products, arithmetic and copies ran while one was open for 0% of the time, Pallas kernels for 1%

profile of v3, /device:TPU:1, one launch (start us, length us, event | category | flops | bytes accessed | tf_op | source)
XLA Modules:
  0.0 76.2 jit_solution(13369421407840009295)
XLA Ops:
  0.6 0.0 copy-start
  0.6 1.4 %copy-done = bf16[64,96,128]{2,1,0:T(8,128)(2,1)S(1)} copy-done((bf16[64,96,128]{2,1,0:T(8,128)(2,1)S(1)}, bf16[64,96,128]{2,1,0:T(8,128)(2,1)}, u32[]{:S(2)}) %copy-start) | copy-done | bytes 1572888
  2.0 0.0 copy-start.2
  2.0 0.6 shard_map.59
  2.6 0.0 copy-start.1
  2.6 4.1 %collective-permute-start.2 = (bf16[8,96,128]{2,1,0:T(8,128)(2,1)S(1)}, bf16[8,96,128]{2,1,0:T(8,128)(2,1)S(1)}, u32[]{:S(2)}, u32[]{:S(2)}) collective-permute-start(bf16[8,96,128]{2,1,0:T(8,128)(2,1)S(1)} %get-tuple-element.14), channel_id=1, source_target_pairs={{0,1},{1,2},{2,3},{3,4},{4,5},{5,6},{6,7},{7,8},{8,9},{9,10},{10,1... | collective-permute-start | bytes 589832 | tf_op jit(solution)/shard_map/ppermute | solution.py:286
  6.7 11.7 %collective-permute-start.3 = (bf16[8,96,128]{2,1,0:T(8,128)(2,1)S(1)}, bf16[8,96,128]{2,1,0:T(8,128)(2,1)S(1)}, u32[]{:S(2)}, u32[]{:S(2)}) collective-permute-start(bf16[8,96,128]{2,1,0:T(8,128)(2,1)S(1)} %get-tuple-element.15), channel_id=1, source_target_pairs={{1,0},{2,1},{3,2},{4,3},{5,4},{6,5},{7,6},{8,7},{9,8},{10,9},{11,1... | collective-permute-start | bytes 589832 | tf_op jit(solution)/shard_map/ppermute | solution.py:286
  18.4 2.1 %collective-permute-start = (bf16[8,8,16,128]{3,2,1,0:T(8,128)(2,1)S(1)}, bf16[8,8,16,128]{3,2,1,0:T(8,128)(2,1)S(1)}, u32[]{:S(2)}, u32[]{:S(2)}) collective-permute-start(bf16[8,8,16,128]{3,2,1,0:T(8,128)(2,1)S(1)} %get-tuple-element.10), channel_id=1, source_target_pairs={{0,32},{32,64},{64,96},{96,128},{128,160},{160,192},{192,224},{224... | collective-permute-start | bytes 786440 | tf_op jit(solution)/shard_map/ppermute | solution.py:286
  20.5 0.0 collective-permute-start.1
  20.5 0.5 collective-permute-done.2.left
  21.0 0.9 %collective-permute-done.3.right = bf16[8,96,128]{2,1,0:T(8,128)(2,1)S(1)} collective-permute-done((bf16[8,96,128]{2,1,0:T(8,128)(2,1)S(1)}, bf16[8,96,128]{2,1,0:T(8,128)(2,1)S(1)}, u32[]{:S(2)}, u32[]{:S(2)}) %collective-permute-start.3) | collective-permute-done | bytes 196640 | tf_op jit(solution)/shard_map/ppermute | solution.py:286
  22.0 2.7 %collective-permute-start.4 = (bf16[16,16,128]{2,1,0:T(8,128)(2,1)S(1)}, bf16[16,16,128]{2,1,0:T(8,128)(2,1)S(1)}, u32[]{:S(2)}, u32[]{:S(2)}) collective-permute-start(bf16[16,16,128]{2,1,0:T(8,128)(2,1)S(1)} %pad_maximum_fusion), channel_id=1, source_target_pairs={{0,32},{32,64},{64,96},{96,128},{128,160},{160,192},{192,224},{224... | collective-permute-start | bytes 196616 | tf_op jit(solution)/shard_map/ppermute | solution.py:286
  24.7 0.0 collective-permute-start.5
  24.7 0.1 pad.12.clone
  24.8 0.0 collective-permute-done.top
  24.8 1.5 %collective-permute-done.1.bottom = bf16[8,8,16,128]{3,2,1,0:T(8,128)(2,1)S(1)} collective-permute-done((bf16[8,8,16,128]{3,2,1,0:T(8,128)(2,1)S(1)}, bf16[8,8,16,128]{3,2,1,0:T(8,128)(2,1)S(1)}, u32[]{:S(2)}, u32[]{:S(2)}) %collective-permute-start.1) | collective-permute-done | bytes 262176 | tf_op jit(solution)/shard_map/ppermute | solution.py:286
  26.3 0.0 copy-done.2
  26.3 1.0 %shard_map.60 = (bf16[8,8,96,128]{3,2,1,0:T(8,128)(2,1)S(1)}, bf16[8,8,96,128]{3,2,1,0:T(8,128)(2,1)S(1)}) custom-call(bf16[8,8,16,128]{3,2,1,0:T(8,128)(2,1)S(1)} %collective-permute-done.top, bf16[8,8,96,128]{3,2,1,0:T(8,128)(2,1)S(1)} %bitcast.13, bf16[8,8,16,128]{3,2,1,0:T(8,128)(2,1)S(1)} %collective-permute-done.1.bottom, bf16[192,128]{1,0:T(8,128)(2,1)S(1)} %copy-done.2), custom_call_target="tpu_custom_call" | custom-call | flops 402653184 | bytes 4718592 | tf_op jit(solution)/shard_map/pallas_call | solution.py:215
  27.3 0.0 collective-permute-done.4.top
  27.3 1.1 %collective-permute-done.5.bottom = bf16[16,16,128]{2,1,0:T(8,128)(2,1)S(1)} collective-permute-done((bf16[16,16,128]{2,1,0:T(8,128)(2,1)S(1)}, bf16[16,16,128]{2,1,0:T(8,128)(2,1)S(1)}, u32[]{:S(2)}, u32[]{:S(2)}) %collective-permute-start.5) | collective-permute-done | bytes 65568 | tf_op jit(solution)/shard_map/ppermute | solution.py:286
  28.4 0.0 copy-done.1
  28.4 5.1 %shard_map.61 = (bf16[128,12288]{1,0:T(8,128)(2,1)S(1)}, f32[64,64]{1,0:T(8,128)S(1)}) custom-call(bf16[8,8,96,128]{3,2,1,0:T(8,128)(2,1)S(1)} %get-tuple-element.12.high, bf16[8,8,96,128]{3,2,1,0:T(8,128)(2,1)S(1)} %get-tuple-element.13.low, bf16[8,96,128]{2,1,0:T(8,128)(2,1)S(1)} %collective-permute-done.2.left, ...), custom_call_target="tpu_custom_call" | custom-call | tf_op jit(solution)/shard_map/pallas_call | solution.py:229
  33.6 0.1 fusion.3
  33.7 0.1 maximum_maximum_fusion.1
  33.7 0.1 broadcast_in_dim.36
  33.8 0.1 broadcast_in_dim.37
  33.9 16.3 %all_to_all.12 = f32[16,1,2176]{2,1,0:T(1,128)S(1)} all-to-all(f32[16,1,2176]{2,1,0:T(1,128)S(1)} %broadcast_in_dim.37), channel_id=1, replica_groups=mesh['row'=16,'col'=32] {'row'}, dimensions={0} | all-to-all | bytes 278528 | tf_op jit(solution)/shard_map/all_to_all | solution.py:279
  50.2 0.1 reduce_sum.28
  50.3 0.1 broadcast_in_dim.38
  50.4 19.5 %all_to_all.13 = f32[32,1,2176]{2,1,0:T(1,128)S(1)} all-to-all(f32[32,1,2176]{2,1,0:T(1,128)S(1)} %broadcast_in_dim.38), channel_id=1, replica_groups=mesh['row'=16,'col'=32] {'col'}, dimensions={0} | all-to-all | bytes 557056 | tf_op jit(solution)/shard_map/all_to_all | solution.py:279
  70.0 0.2 reduce_sum.29
  70.2 0.1 reshape.25
  70.2 0.1 slice.44
  70.3 0.1 copy.17
  70.4 0.1 bitcast_select_fusion.1
  70.5 0.1 copy.22
  70.5 0.1 maximum_maximum_fusion.gram
  70.6 5.6 %shard_map.62 = (f32[64,96,128]{2,1,0:T(8,128)}, f32[64,64]{1,0:T(8,128)}) custom-call(f32[64,64]{1,0:T(8,128)S(1)} %maximum_maximum_fusion.gram, bf16[128,12288]{1,0:T(8,128)(2,1)S(1)} %get-tuple-element.17.field), custom_call_target="tpu_custom_call" | custom-call | tf_op jit(solution)/shard_map/pallas_call | solution.py:241
  (6 shorter events, 0.0 us)
Async XLA Ops:
  0.6 1.4 %copy-start = (bf16[64,96,128]{2,1,0:T(8,128)(2,1)S(1)}, bf16[64,96,128]{2,1,0:T(8,128)(2,1)}, u32[]{:S(2)}) copy-start(bf16[64,96,128]{2,1,0:T(8,128)(2,1)} %param.4) | copy-start | bytes 4718596
  2.0 24.3 %copy-start.2 = (bf16[192,128]{1,0:T(8,128)(2,1)S(1)}, bf16[192,128]{1,0:T(8,128)(2,1)}, u32[]{:S(2)}) copy-start(bf16[192,128]{1,0:T(8,128)(2,1)} %constant.4.clone.weights) | copy-start | bytes 147460
  2.6 25.8 %copy-start.1 = (bf16[8,256,256]{2,1,0:T(8,128)(2,1)S(1)}, bf16[8,256,256]{2,1,0:T(8,128)(2,1)}, u32[]{:S(2)}) copy-start(bf16[8,256,256]{2,1,0:T(8,128)(2,1)} %constant.10.clone.across) | copy-start | bytes 3145732
  2.6 18.4 %collective-permute-start.2 = (bf16[8,96,128]{2,1,0:T(8,128)(2,1)S(1)}, bf16[8,96,128]{2,1,0:T(8,128)(2,1)S(1)}, u32[]{:S(2)}, u32[]{:S(2)}) collective-permute-start(bf16[8,96,128]{2,1,0:T(8,128)(2,1)S(1)} %get-tuple-element.14), channel_id=1, source_target_pairs={{0,1},{1,2},{2,3},{3,4},{4,5},{5,6},{6,7},{7,8},{8,9},{9,10},{10,1... | collective-permute-start | bytes 589832 | tf_op jit(solution)/shard_map/ppermute | solution.py:286
  6.7 15.2 %collective-permute-start.3 = (bf16[8,96,128]{2,1,0:T(8,128)(2,1)S(1)}, bf16[8,96,128]{2,1,0:T(8,128)(2,1)S(1)}, u32[]{:S(2)}, u32[]{:S(2)}) collective-permute-start(bf16[8,96,128]{2,1,0:T(8,128)(2,1)S(1)} %get-tuple-element.15), channel_id=1, source_target_pairs={{1,0},{2,1},{3,2},{4,3},{5,4},{6,5},{7,6},{8,7},{9,8},{10,9},{11,1... | collective-permute-start | bytes 589832 | tf_op jit(solution)/shard_map/ppermute | solution.py:286
  18.4 6.4 %collective-permute-start = (bf16[8,8,16,128]{3,2,1,0:T(8,128)(2,1)S(1)}, bf16[8,8,16,128]{3,2,1,0:T(8,128)(2,1)S(1)}, u32[]{:S(2)}, u32[]{:S(2)}) collective-permute-start(bf16[8,8,16,128]{3,2,1,0:T(8,128)(2,1)S(1)} %get-tuple-element.10), channel_id=1, source_target_pairs={{0,32},{32,64},{64,96},{96,128},{128,160},{160,192},{192,224},{224... | collective-permute-start | bytes 786440 | tf_op jit(solution)/shard_map/ppermute | solution.py:286
  20.5 5.8 %collective-permute-start.1 = (bf16[8,8,16,128]{3,2,1,0:T(8,128)(2,1)S(1)}, bf16[8,8,16,128]{3,2,1,0:T(8,128)(2,1)S(1)}, u32[]{:S(2)}, u32[]{:S(2)}) collective-permute-start(bf16[8,8,16,128]{3,2,1,0:T(8,128)(2,1)S(1)} %get-tuple-element.11), channel_id=1, source_target_pairs={{32,0},{64,32},{96,64},{128,96},{160,128},{192,160},{224,192},{256... | collective-permute-start | bytes 786440 | tf_op jit(solution)/shard_map/ppermute | solution.py:286
  22.0 5.3 %collective-permute-start.4 = (bf16[16,16,128]{2,1,0:T(8,128)(2,1)S(1)}, bf16[16,16,128]{2,1,0:T(8,128)(2,1)S(1)}, u32[]{:S(2)}, u32[]{:S(2)}) collective-permute-start(bf16[16,16,128]{2,1,0:T(8,128)(2,1)S(1)} %pad_maximum_fusion), channel_id=1, source_target_pairs={{0,32},{32,64},{64,96},{96,128},{128,160},{160,192},{192,224},{224... | collective-permute-start | bytes 196616 | tf_op jit(solution)/shard_map/ppermute | solution.py:286
  24.7 3.7 %collective-permute-start.5 = (bf16[16,16,128]{2,1,0:T(8,128)(2,1)S(1)}, bf16[16,16,128]{2,1,0:T(8,128)(2,1)S(1)}, u32[]{:S(2)}, u32[]{:S(2)}) collective-permute-start(bf16[16,16,128]{2,1,0:T(8,128)(2,1)S(1)} %pad_maximum_fusion.1), channel_id=1, source_target_pairs={{32,0},{64,32},{96,64},{128,96},{160,128},{192,160},{224,192},{256... | collective-permute-start | bytes 196616 | tf_op jit(solution)/shard_map/ppermute | solution.py:286

commit v4 on v3

--- a/solution.py
+++ b/solution.py
@@ -7,10 +7,12 @@
 from jax.experimental.pallas import tpu as pltpu
 from jax.sharding import PartitionSpec as P
 
+
 HALF = 16
 TAPS = 2 * HALF + 1
 BF16, F32 = jnp.bfloat16, jnp.float32
 STEP = 48
+PAD = 8
 
 
 def band(length):
@@ -30,8 +32,30 @@
     return high, low
 
 
-def row_weights(height):
-    return np.concatenate([part.T for part in two(band(height))], axis=0)
+def row_weights(row, col):
+    sigma = HALF / 3.0
+    offsets = np.arange(TAPS) - HALF
+    total = float(np.exp(-offsets * offsets / (2.0 * sigma * sigma)).sum())
+    spread = col - row
+    shifted = (spread - HALF).astype(F32)
+    value = jnp.exp(shifted * shifted * (-0.5 / (sigma * sigma))) * (1.0 / total)
+    value = jnp.where((spread >= 0) & (spread <= 2 * HALF), value, 0.0)
+    return jnp.concatenate(split(value), axis=0)
+
+
+def indices(rows, cols):
+    return [lax.broadcasted_iota(jnp.int32, (rows, cols), i) for i in range(2)]
+
+
+def edge_column_weights(width):
+    matrix = band(width)
+    edge = np.r_[width - HALF : width, :HALF]
+    left, right = matrix[:HALF, edge], matrix[HALF + width :, edge]
+    result = []
+    for pair in ((left, right), (right, left)):
+        block = np.concatenate(pair, axis=0)
+        result.append(np.concatenate(two(np.kron(np.eye(4), block)), axis=1))
+    return np.stack(result)
 
 
 def column_weights(width):
@@ -81,28 +105,31 @@
     first_rows[...] = own[:, :, :HALF, :]
 
 
-def rows_kernel(top, own, bottom, weights, high, low):
+def rows_kernel(top, own, bottom, high, low):
     height, width = own.shape[2:]
+    weights = row_weights(*indices(height, height + 2 * HALF))
     for g in range(8):
         for k in range(0, 8, 2):
             parts = [jnp.concatenate([top[g, i], own[g, i], bottom[g, i]], axis=0) for i in (k, k + 1)]
-            both = dot(weights[...], jnp.concatenate(parts, axis=1))
+            both = dot(weights, jnp.concatenate(parts, axis=1))
             upper, lower = split(both[:height] + both[height:])
             high[g, k], high[g, k + 1] = upper[:, :width], upper[:, width:]
             low[g, k], low[g, k + 1] = lower[:, :width], lower[:, width:]
 
 
-def columns_kernel(points, high, low, left, right, top, bottom, weights, across, field, packed, halo_high, halo_low, flat):
+def mixed(a, b):
+    lane = lax.broadcasted_iota(jnp.int32, a.shape, 1)
+    even = (lane // HALF) % 2 == 0
+    a, b = a.astype(F32), b.astype(F32)
+    return jnp.concatenate([jnp.where(even, a, b), jnp.where(even, b, a)], axis=1).astype(BF16)
+
+
+def columns_kernel(high, low, left, right, across, flat, halo_high, halo_low):
     height, width = high.shape[2:]
-    lane = lax.broadcasted_iota(jnp.int32, (height + 2 * HALF, width), 1)
-    even = (lane // HALF) % 2 == 0
+    row, col = indices(height, height)
+    weights = row_weights(row, col + HALF)
     for g in range(8):
-        a, b = [
-            jnp.concatenate([top[i], side[g], bottom[i]], axis=0).astype(F32)
-            for side, i in ((left, g), (right, 8 + g))
-        ]
-        both = jnp.concatenate([jnp.where(even, a, b), jnp.where(even, b, a)], axis=1).astype(BF16)
-        both = dot(weights[...], both)
+        both = dot(weights, mixed(left[g], right[g]))
         upper, lower = split(both[:height] + both[height:])
         halo_high[g], halo_low[g] = upper, lower
     for k in range(8):
@@ -112,10 +139,45 @@
             lower = jnp.concatenate([low[g, k], halo_low[g, :, lanes]], axis=1)
             both = dot(upper, across[k])
             value = both[:, :width] + both[:, width:] + dot(lower, across[k, :, :width])
-            flat[pl.ds((8 * g + k) * (height + 8), height), :] = value
-    count = 64
+            flat[pl.ds((8 * g + k) * (height + PAD), height), :] = value
+
+
+def gram_kernel(points, height, flat, top, bottom, across, field, gram, edge):
+    width, count, pitch, band_rows = flat.shape[1], 64, height + PAD, 2 * HALF + PAD
+    row, col = indices(2 * HALF, 2 * HALF)
+    row = jnp.where(row < HALF, row, row + height - 2 * HALF)
+    col = jnp.where(col < HALF, col, col + height)
+    weights = row_weights(row, col)
+    uppers, lowers = [], []
+    for g in range(8):
+        a, b = [jnp.concatenate([top[i], bottom[i]], axis=0) for i in (g, 8 + g)]
+        both = dot(weights, mixed(a, b))
+        upper, lower = split(both[: 2 * HALF] + both[2 * HALF :])
+        uppers.append(upper)
+        lowers.append(lower)
+    upper, lower = jnp.concatenate(uppers, axis=0), jnp.concatenate(lowers, axis=0)
+    lane = lax.broadcasted_iota(jnp.int32, (2 * HALF, width), 1)
+    inside = (lane < HALF) | (lane >= width - HALF)
+    for h in range(2):
+        lanes = slice(width * h, width * (h + 1))
+        both = dot(upper[:, lanes], across[h])
+        value = both[:, :width] + both[:, width:] + dot(lower[:, lanes], across[h, :, :width])
+        for g in range(8):
+            rows = value[2 * HALF * g : 2 * HALF * (g + 1)]
+            for q in range(4):
+                s = 8 * g + 4 * h + q
+                added = jnp.where(inside, pltpu.roll(rows, width - HALF - 2 * HALF * q, 1), 0.0)
+                edge[pl.ds(s * band_rows, HALF), :] = flat[pl.ds(s * pitch, HALF), :] + added[:HALF]
+                edge[pl.ds(s * band_rows + HALF, HALF), :] = (
+                    flat[pl.ds(s * pitch + height - HALF, HALF), :] + added[HALF:]
+                )
     for r in range(height):
-        upper, lower = split(flat[pl.ds(r, count, stride=height + 8), :])
+        if HALF <= r < height - HALF:
+            value = flat[pl.ds(r, count, stride=pitch), :]
+        else:
+            start = r if r < HALF else r - height + 2 * HALF
+            value = edge[pl.ds(start, count, stride=band_rows), :]
+        upper, lower = split(value)
         field[:count, r * width : (r + 1) * width] = upper
         field[count:, r * width : (r + 1) * width] = lower
     total = jnp.zeros((2 * count, 2 * count), F32)
@@ -123,8 +185,8 @@
     for start in range(0, height * width, size):
         part = field[:, start : start + size]
         total = total + lax.dot_general(part, part, (((1,), (1,)), ((), ())), preferred_element_type=F32)
-    gram = total[:count, :count] + total[count:, count:] + (total[:count, count:] + total[count:, :count])
-    packed[...] = gram / points
+    total = total[:count, :count] + total[count:, count:] + (total[:count, count:] + total[count:, :count])
+    gram[...] = total / points
 
 
 def factor(gram, size=8):
@@ -215,25 +277,40 @@
     return pl.pallas_call(
         rows_kernel,
         out_shape=[shape(8, 8, height, width)] * 2,
-        in_specs=whole(4),
+        in_specs=whole(3),
         out_specs=whole(2),
         compiler_params=pltpu.CompilerParams(vmem_limit_bytes=16 << 20),
         cost_estimate=pl.CostEstimate(
             flops=4 * own.size * (height + 2 * HALF), bytes_accessed=6 * own.size, transcendentals=0
         ),
-    )(top, own, bottom, jnp.asarray(row_weights(height)))
-
-
-def filter_columns(high, low, sides, points):
+    )(top, own, bottom)
+
+
+def filter_columns(high, low, left, right):
     height, width = high.shape[2:]
     return pl.pallas_call(
-        functools.partial(columns_kernel, points),
+        columns_kernel,
+        out_shape=shape(64 * (height + PAD), width, dtype=F32),
+        in_specs=whole(5),
+        out_specs=whole(1)[0],
+        compiler_params=pltpu.CompilerParams(vmem_limit_bytes=16 << 20),
+        scratch_shapes=[pltpu.VMEM((8, height, 2 * width), BF16)] * 2,
+        cost_estimate=pl.CostEstimate(
+            flops=12 * width * high.size, bytes_accessed=8 * high.size, transcendentals=0
+        ),
+    )(high, low, left, right, jnp.asarray(column_weights(width)))
+
+
+def correlate(flat, top, bottom, height, points):
+    width = flat.shape[1]
+    return pl.pallas_call(
+        functools.partial(gram_kernel, points, height),
         out_shape=[shape(128, height * width), shape(64, 64, dtype=F32)],
-        in_specs=whole(8),
+        in_specs=whole(4),
         out_specs=whole(2),
-        compiler_params=pltpu.CompilerParams(vmem_limit_bytes=24 << 20),
-        scratch_shapes=[pltpu.VMEM((8, height, 2 * width), BF16)] * 2 + [pltpu.VMEM((64 * (height + 8), width), F32)],
-    )(high, low, *sides, jnp.asarray(row_weights(height)), jnp.asarray(column_weights(width)))
+        compiler_params=pltpu.CompilerParams(vmem_limit_bytes=16 << 20),
+        scratch_shapes=[pltpu.VMEM((64 * (2 * HALF + PAD), width), F32)],
+    )(flat, top, bottom, jnp.asarray(edge_column_weights(width)))
 
 
 def orthonormal(gram, field, height, width):
@@ -283,10 +360,12 @@
     devices = lax.axis_size(axis)
     up = [(i, (i + 1) % devices) for i in range(devices)]
     down = [(j, i) for i, j in up]
-    return lax.ppermute(upward, axis, up), lax.ppermute(downward, axis, down)
-
-
-def local(snapshots):
+    first = lax.ppermute(upward, axis, up)
+    second = lax.ppermute(downward, axis, down)
+    return first, second
+
+
+def program(snapshots):
     count, height, width = snapshots.shape
     points = height * width * lax.axis_size("row") * lax.axis_size("col")
     own = snapshots.reshape(8, 8, height, width)
@@ -298,7 +377,8 @@
     ]
     corners = swap(last_rows, first_rows, "row")
     high, low = filter_rows(top, own, bottom)
-    field, gram = filter_columns(high, low, (*sides, *corners), points)
+    flat = filter_columns(high, low, *sides)
+    field, gram = correlate(flat, *corners, height, points)
     total = pack(gram).reshape(-1)
     total = summed(summed(total, "row"), "col")
     gram = unpack(total.reshape(count // 2 + 2, count))
@@ -307,7 +387,7 @@
 
 def solution(mesh):
     return jax.shard_map(
-        local,
+        program,
         mesh=mesh,
         in_specs=(P(None, "row", "col"),),
         out_specs=(P(None, "row", "col"), P()),

time: 76.4 us -> 76.5 us (level)
  blocking collectives: 35.8 us -> 37.4 us
  waiting for transfers between devices: 4.02 us -> 2.85 us
  Pallas kernels: 12.2 us -> 11.4 us
    all_to_all x2, blocking collectives: 35.8 us -> 37.4 us  [summed(): return lax.all_to_all(copies, axis, 0, 0).sum(0)]
    ppermute x6, waiting for transfers between devices: 4.02 us -> 2.85 us  [the longest x3 2.13 us: swap(): second = lax.ppermute(downward, axis, down)]
    pallas_call x1 -> x2, Pallas kernels: 5.14 us -> 4.25 us  [the longest x1 2.31 us: filter_columns(): pl.pallas_call(columns_kernel, out_shape=shape(64 * (height + PAD), width...]
  transfers between devices with their start and end apart: 6 -> 6, of which waited for: 4 -> 3; matrix products, arithmetic and copies ran while one was open for 0% -> 0% of each run, Pallas kernels for 1% -> 4%
where the time goes in v4:
time: 76.5 us; the launch traced here: 76.2 us
  blocking collectives  37.4 us (49%)
  starting transfers between devices  21.2 us (28%)
  Pallas kernels  11.4 us (15%)
  waiting for transfers between devices  2.85 us (4%)
  local copies, waits for them, and re-layouts  2.1 us (3%)
  between operations  0.77 us (1%)
    all_to_all x2, blocking collectives, summed(): return lax.all_to_all(copies, axis, 0, 0).sum(0)  37.4 us
    ppermute x3, starting transfers between devices, swap(): second = lax.ppermute(downward, axis, down)  11.4 us
    ppermute x3, starting transfers between devices, swap(): first = lax.ppermute(upward, axis, up)  9.78 us
    pallas_call x1, Pallas kernels, orthonormal(): pl.pallas_call(basis_kernel, grid=(height // STEP,), compiler_params=pltp...  5.56 us
    pallas_call x1, Pallas kernels, filter_columns(): pl.pallas_call(columns_kernel, out_shape=shape(64 * (height + PAD), width...  2.31 us
    ppermute x3, waiting for transfers between devices, swap(): second = lax.ppermute(downward, axis, down)  2.13 us
    pallas_call x1, Pallas kernels, correlate(): pl.pallas_call(functools.partial(gram_kernel, points, height), out_shape=...  1.94 us
  transfers between devices with their start and end apart: 6, of which 3 were waited for; matrix products, arithmetic and copies ran while one was open for 0% of the time, Pallas kernels for 4%

profile of v4, /device:TPU:1, one launch (start us, length us, event | category | flops | bytes accessed | tf_op | source)
XLA Modules:
  0.0 76.2 jit_solution(8495167180472668358)
XLA Ops:
  0.6 0.0 copy-start
  0.6 1.4 %copy-done = bf16[64,96,128]{2,1,0:T(8,128)(2,1)S(1)} copy-done((bf16[64,96,128]{2,1,0:T(8,128)(2,1)S(1)}, bf16[64,96,128]{2,1,0:T(8,128)(2,1)}, u32[]{:S(2)}) %copy-start) | copy-done | bytes 1572888
  2.0 0.0 copy-start.1
  2.0 0.6 shard_map.50
  2.6 3.9 %collective-permute-start.2 = (bf16[8,96,128]{2,1,0:T(8,128)(2,1)S(1)}, bf16[8,96,128]{2,1,0:T(8,128)(2,1)S(1)}, u32[]{:S(2)}, u32[]{:S(2)}) collective-permute-start(bf16[8,96,128]{2,1,0:T(8,128)(2,1)S(1)} %get-tuple-element.14), channel_id=1, source_target_pairs={{0,1},{1,2},{2,3},{3,4},{4,5},{5,6},{6,7},{7,8},{8,9},{9,10},{10,1... | collective-permute-start | bytes 589832 | tf_op jit(solution)/shard_map/ppermute | solution.py:363
  6.6 2.1 %collective-permute-start = (bf16[8,8,16,128]{3,2,1,0:T(8,128)(2,1)S(1)}, bf16[8,8,16,128]{3,2,1,0:T(8,128)(2,1)S(1)}, u32[]{:S(2)}, u32[]{:S(2)}) collective-permute-start(bf16[8,8,16,128]{3,2,1,0:T(8,128)(2,1)S(1)} %get-tuple-element.10), channel_id=1, source_target_pairs={{0,32},{32,64},{64,96},{96,128},{128,160},{160,192},{192,224},{224... | collective-permute-start | bytes 786440 | tf_op jit(solution)/shard_map/ppermute | solution.py:363
  8.7 2.7 %collective-permute-start.1 = (bf16[8,8,16,128]{3,2,1,0:T(8,128)(2,1)S(1)}, bf16[8,8,16,128]{3,2,1,0:T(8,128)(2,1)S(1)}, u32[]{:S(2)}, u32[]{:S(2)}) collective-permute-start(bf16[8,8,16,128]{3,2,1,0:T(8,128)(2,1)S(1)} %get-tuple-element.11), channel_id=1, source_target_pairs={{32,0},{64,32},{96,64},{128,96},{160,128},{192,160},{224,192},{256... | collective-permute-start | bytes 786440 | tf_op jit(solution)/shard_map/ppermute | solution.py:364
  11.4 8.7 %collective-permute-start.3 = (bf16[8,96,128]{2,1,0:T(8,128)(2,1)S(1)}, bf16[8,96,128]{2,1,0:T(8,128)(2,1)S(1)}, u32[]{:S(2)}, u32[]{:S(2)}) collective-permute-start(bf16[8,96,128]{2,1,0:T(8,128)(2,1)S(1)} %get-tuple-element.15), channel_id=1, source_target_pairs={{1,0},{2,1},{3,2},{4,3},{5,4},{6,5},{7,6},{8,7},{9,8},{10,9},{11,1... | collective-permute-start | bytes 589832 | tf_op jit(solution)/shard_map/ppermute | solution.py:364
  20.1 0.1 pad.12.clone
  20.2 0.7 collective-permute-done.2.left
  20.9 1.8 %collective-permute-done.3.right = bf16[8,96,128]{2,1,0:T(8,128)(2,1)S(1)} collective-permute-done((bf16[8,96,128]{2,1,0:T(8,128)(2,1)S(1)}, bf16[8,96,128]{2,1,0:T(8,128)(2,1)S(1)}, u32[]{:S(2)}, u32[]{:S(2)}) %collective-permute-start.3) | collective-permute-done | bytes 196640 | tf_op jit(solution)/shard_map/ppermute | solution.py:364
  22.7 3.7 %collective-permute-start.4 = (bf16[16,16,128]{2,1,0:T(8,128)(2,1)S(1)}, bf16[16,16,128]{2,1,0:T(8,128)(2,1)S(1)}, u32[]{:S(2)}, u32[]{:S(2)}) collective-permute-start(bf16[16,16,128]{2,1,0:T(8,128)(2,1)S(1)} %pad_maximum_fusion), channel_id=1, source_target_pairs={{0,32},{32,64},{64,96},{96,128},{128,160},{160,192},{192,224},{224... | collective-permute-start | bytes 196616 | tf_op jit(solution)/shard_map/ppermute | solution.py:363
  26.4 0.0 collective-permute-start.5
  26.4 0.0 collective-permute-done.top
  26.5 0.0 collective-permute-done.1.bottom
  26.5 1.0 %shard_map.51 = (bf16[8,8,96,128]{3,2,1,0:T(8,128)(2,1)S(1)}, bf16[8,8,96,128]{3,2,1,0:T(8,128)(2,1)S(1)}) custom-call(bf16[8,8,16,128]{3,2,1,0:T(8,128)(2,1)S(1)} %collective-permute-done.top, bf16[8,8,96,128]{3,2,1,0:T(8,128)(2,1)S(1)} %bitcast.13, bf16[8,8,16,128]{3,2,1,0:T(8,128)(2,1)S(1)} %collective-permute-done.1.bottom), custom_call_target="tpu_custom_call" | custom-call | flops 402653184 | bytes 4718592 | tf_op jit(solution)/shard_map/pallas_call | solution.py:277
  27.4 0.0 copy-done.1
  27.4 0.0 copy-start.2
  27.5 2.3 %shard_map.52.flat = f32[6656,128]{1,0:T(8,128)S(1)} custom-call(bf16[8,8,96,128]{3,2,1,0:T(8,128)(2,1)S(1)} %get-tuple-element.12.high, bf16[8,8,96,128]{3,2,1,0:T(8,128)(2,1)S(1)} %get-tuple-element.13.low, bf16[8,96,128]{2,1,0:T(8,128)(2,1)S(1)} %collective-permute-done.2.left, bf16[8,96,128]{2,1,0:T(8,128)(2,1)S(1)} %collective-permute-done.3.right, ...), custom_call_target="tpu_custom_call" | custom-call | flops 1207959552 | bytes 6291456 | tf_op jit(solution)/shard_map/pallas_call | solution.py:291
  29.8 0.0 collective-permute-done.4.top
  29.8 0.3 collective-permute-done.5.bottom
  30.1 0.0 copy-done.2
  30.1 1.9 %shard_map.53 = (bf16[128,12288]{1,0:T(8,128)(2,1)S(1)}, f32[64,64]{1,0:T(8,128)S(1)}) custom-call(f32[6656,128]{1,0:T(8,128)S(1)} %shard_map.52.flat, bf16[16,16,128]{2,1,0:T(8,128)(2,1)S(1)} %collective-permute-done.4.top, bf16[16,16,128]{2,1,0:T(8,128)(2,1)S(1)} %collective-permute-done.5.bottom, bf16[2,128,256]{2,1,0:T(8,128)(2,1)S(1)} %copy-done.2), custom_call_target="tpu_custom_call" | custom-call | tf_op jit(solution)/shard_map/pallas_call | solution.py:306
  32.1 0.1 fusion.3
  32.2 0.1 maximum_maximum_fusion.1
  32.2 0.1 broadcast_in_dim.36
  32.3 0.1 broadcast_in_dim.37
  32.4 17.5 %all_to_all.12 = f32[16,1,2176]{2,1,0:T(1,128)S(1)} all-to-all(f32[16,1,2176]{2,1,0:T(1,128)S(1)} %broadcast_in_dim.37), channel_id=1, replica_groups=mesh['row'=16,'col'=32] {'row'}, dimensions={0} | all-to-all | bytes 278528 | tf_op jit(solution)/shard_map/all_to_all | solution.py:356
  49.9 0.1 reduce_sum.28
  50.0 0.1 broadcast_in_dim.38
  50.2 19.8 %all_to_all.13 = f32[32,1,2176]{2,1,0:T(1,128)S(1)} all-to-all(f32[32,1,2176]{2,1,0:T(1,128)S(1)} %broadcast_in_dim.38), channel_id=1, replica_groups=mesh['row'=16,'col'=32] {'col'}, dimensions={0} | all-to-all | bytes 557056 | tf_op jit(solution)/shard_map/all_to_all | solution.py:356
  70.0 0.2 reduce_sum.29
  70.2 0.1 reshape.25
  70.3 0.1 slice.44
  70.4 0.1 copy.16
  70.4 0.1 bitcast_select_fusion.1
  70.5 0.1 copy.21
  70.6 0.1 maximum_maximum_fusion.gram
  70.7 5.6 %shard_map.54 = (f32[64,96,128]{2,1,0:T(8,128)}, f32[64,64]{1,0:T(8,128)}) custom-call(f32[64,64]{1,0:T(8,128)S(1)} %maximum_maximum_fusion.gram, bf16[128,12288]{1,0:T(8,128)(2,1)S(1)} %get-tuple-element.17.field), custom_call_target="tpu_custom_call" | custom-call | tf_op jit(solution)/shard_map/pallas_call | solution.py:318
  (6 shorter events, 0.0 us)
Async XLA Ops:
  0.6 1.4 %copy-start = (bf16[64,96,128]{2,1,0:T(8,128)(2,1)S(1)}, bf16[64,96,128]{2,1,0:T(8,128)(2,1)}, u32[]{:S(2)}) copy-start(bf16[64,96,128]{2,1,0:T(8,128)(2,1)} %param.3) | copy-start | bytes 4718596
  2.0 25.4 %copy-start.1 = (bf16[8,256,256]{2,1,0:T(8,128)(2,1)S(1)}, bf16[8,256,256]{2,1,0:T(8,128)(2,1)}, u32[]{:S(2)}) copy-start(bf16[8,256,256]{2,1,0:T(8,128)(2,1)} %constant.4.clone.across) | copy-start | bytes 3145732
  2.6 18.3 %collective-permute-start.2 = (bf16[8,96,128]{2,1,0:T(8,128)(2,1)S(1)}, bf16[8,96,128]{2,1,0:T(8,128)(2,1)S(1)}, u32[]{:S(2)}, u32[]{:S(2)}) collective-permute-start(bf16[8,96,128]{2,1,0:T(8,128)(2,1)S(1)} %get-tuple-element.14), channel_id=1, source_target_pairs={{0,1},{1,2},{2,3},{3,4},{4,5},{5,6},{6,7},{7,8},{8,9},{9,10},{10,1... | collective-permute-start | bytes 589832 | tf_op jit(solution)/shard_map/ppermute | solution.py:363
  6.6 19.9 %collective-permute-start = (bf16[8,8,16,128]{3,2,1,0:T(8,128)(2,1)S(1)}, bf16[8,8,16,128]{3,2,1,0:T(8,128)(2,1)S(1)}, u32[]{:S(2)}, u32[]{:S(2)}) collective-permute-start(bf16[8,8,16,128]{3,2,1,0:T(8,128)(2,1)S(1)} %get-tuple-element.10), channel_id=1, source_target_pairs={{0,32},{32,64},{64,96},{96,128},{128,160},{160,192},{192,224},{224... | collective-permute-start | bytes 786440 | tf_op jit(solution)/shard_map/ppermute | solution.py:363
  8.7 17.7 %collective-permute-start.1 = (bf16[8,8,16,128]{3,2,1,0:T(8,128)(2,1)S(1)}, bf16[8,8,16,128]{3,2,1,0:T(8,128)(2,1)S(1)}, u32[]{:S(2)}, u32[]{:S(2)}) collective-permute-start(bf16[8,8,16,128]{3,2,1,0:T(8,128)(2,1)S(1)} %get-tuple-element.11), channel_id=1, source_target_pairs={{32,0},{64,32},{96,64},{128,96},{160,128},{192,160},{224,192},{256... | collective-permute-start | bytes 786440 | tf_op jit(solution)/shard_map/ppermute | solution.py:364
  11.4 11.3 %collective-permute-start.3 = (bf16[8,96,128]{2,1,0:T(8,128)(2,1)S(1)}, bf16[8,96,128]{2,1,0:T(8,128)(2,1)S(1)}, u32[]{:S(2)}, u32[]{:S(2)}) collective-permute-start(bf16[8,96,128]{2,1,0:T(8,128)(2,1)S(1)} %get-tuple-element.15), channel_id=1, source_target_pairs={{1,0},{2,1},{3,2},{4,3},{5,4},{6,5},{7,6},{8,7},{9,8},{10,9},{11,1... | collective-permute-start | bytes 589832 | tf_op jit(solution)/shard_map/ppermute | solution.py:364
  22.7 7.1 %collective-permute-start.4 = (bf16[16,16,128]{2,1,0:T(8,128)(2,1)S(1)}, bf16[16,16,128]{2,1,0:T(8,128)(2,1)S(1)}, u32[]{:S(2)}, u32[]{:S(2)}) collective-permute-start(bf16[16,16,128]{2,1,0:T(8,128)(2,1)S(1)} %pad_maximum_fusion), channel_id=1, source_target_pairs={{0,32},{32,64},{64,96},{96,128},{128,160},{160,192},{192,224},{224... | collective-permute-start | bytes 196616 | tf_op jit(solution)/shard_map/ppermute | solution.py:363
  26.4 3.7 %collective-permute-start.5 = (bf16[16,16,128]{2,1,0:T(8,128)(2,1)S(1)}, bf16[16,16,128]{2,1,0:T(8,128)(2,1)S(1)}, u32[]{:S(2)}, u32[]{:S(2)}) collective-permute-start(bf16[16,16,128]{2,1,0:T(8,128)(2,1)S(1)} %pad_maximum_fusion.1), channel_id=1, source_target_pairs={{32,0},{64,32},{96,64},{128,96},{160,128},{192,160},{224,192},{256... | collective-permute-start | bytes 196616 | tf_op jit(solution)/shard_map/ppermute | solution.py:364
  27.4 2.7 %copy-start.2 = (bf16[2,128,256]{2,1,0:T(8,128)(2,1)S(1)}, bf16[2,128,256]{2,1,0:T(8,128)(2,1)}, u32[]{:S(2)}) copy-start(bf16[2,128,256]{2,1,0:T(8,128)(2,1)} %constant.10.clone.across) | copy-start | bytes 393220

commit v5 on v4

--- a/solution.py
+++ b/solution.py
@@ -186,7 +186,14 @@
         part = field[:, start : start + size]
         total = total + lax.dot_general(part, part, (((1,), (1,)), ((), ())), preferred_element_type=F32)
     total = total[:count, :count] + total[count:, count:] + (total[:count, count:] + total[count:, :count])
-    gram[...] = total / points
+    total = total / points
+    half = count // 2
+    row, col = indices(half, half)
+    second = total[half:, half:]
+    diagonal = jnp.sum(jnp.where(row == col, second, 0.0), axis=0, keepdims=True)
+    gram[:half, :] = jnp.concatenate([jnp.where(row <= col, total[:half, :half], second), total[:half, half:]], axis=1)
+    gram[half : half + 1, :] = jnp.concatenate([diagonal, jnp.zeros_like(diagonal)], axis=1)
+    gram[half + 1 :, :] = jnp.zeros((1, count), F32)
 
 
 def factor(gram, size=8):
@@ -227,12 +234,24 @@
     return rows
 
 
+def unpack(packed):
+    half = packed.shape[1] // 2
+    mixture, cross, diagonal = packed[:half, :half], packed[:half, half:], packed[half : half + 1, :half]
+    row, col = indices(half, half)
+    other = mixture.T
+    first = jnp.where(row <= col, mixture, other)
+    second = jnp.where(row > col, mixture, other)
+    second = jnp.where(row == col, diagonal, second)
+    top = jnp.concatenate([first, cross], axis=1)
+    return jnp.concatenate([top, jnp.concatenate([cross.T, second], axis=1)], axis=0)
+
+
 def basis_kernel(gram, field, basis, upper, work, inverse):
-    count = gram.shape[0]
+    count = gram.shape[1]
 
     @pl.when(pl.program_id(0) == 0)
     def _():
-        for k, value in enumerate(factor(gram[...])):
+        for k, value in enumerate(factor(unpack(gram[...]))):
             work[k : k + 1, :] = value
         row = lax.broadcasted_iota(jnp.int32, (count, count), 0)
         col = lax.broadcasted_iota(jnp.int32, (count, count), 1)
@@ -305,7 +324,7 @@
     width = flat.shape[1]
     return pl.pallas_call(
         functools.partial(gram_kernel, points, height),
-        out_shape=[shape(128, height * width), shape(64, 64, dtype=F32)],
+        out_shape=[shape(128, height * width), shape(34, 64, dtype=F32)],
         in_specs=whole(4),
         out_specs=whole(2),
         compiler_params=pltpu.CompilerParams(vmem_limit_bytes=16 << 20),
@@ -314,41 +333,16 @@
 
 
 def orthonormal(gram, field, height, width):
-    count = gram.shape[0]
+    count = gram.shape[1]
     return pl.pallas_call(
         basis_kernel,
         grid=(height // STEP,),
         compiler_params=pltpu.CompilerParams(vmem_limit_bytes=24 << 20),
         out_shape=[shape(count, height, width, dtype=F32), shape(count, count, dtype=F32)],
-        in_specs=[pl.BlockSpec((count, count), lambda i: (0, 0)), pl.BlockSpec((2 * count, STEP * width), lambda i: (0, i))],
+        in_specs=[pl.BlockSpec(gram.shape, lambda i: (0, 0)), pl.BlockSpec((2 * count, STEP * width), lambda i: (0, i))],
         out_specs=[pl.BlockSpec((count, STEP, width), lambda i: (0, i, 0)), pl.BlockSpec((count, count), lambda i: (0, 0))],
         scratch_shapes=[pltpu.VMEM((count, 2 * count), F32), pltpu.VMEM((2 * count, 2 * count), BF16)],
     )(gram, field)
-
-
-def pack(gram):
-    half = gram.shape[0] // 2
-    first, second = gram[:half, :half], gram[half:, half:]
-    row = lax.broadcasted_iota(jnp.int32, (half, half), 0)
-    col = lax.broadcasted_iota(jnp.int32, (half, half), 1)
-    mixed = jnp.where(row >= col, first, second)
-    diagonal = jnp.sum(jnp.where(row == col, second, 0.0), axis=0)
-    diagonal = jnp.pad(diagonal, (0, half))[None]
-    top = jnp.concatenate([gram[half:, :half], mixed], axis=1)
-    return jnp.concatenate([top, diagonal, jnp.zeros_like(diagonal)], axis=0)
-
-
-def unpack(packed):
-    half = packed.shape[1] // 2
-    cross, mixed, diagonal = packed[:half, :half], packed[:half, half:], packed[half, :half]
-    row = lax.broadcasted_iota(jnp.int32, (half, half), 0)
-    col = lax.broadcasted_iota(jnp.int32, (half, half), 1)
-    first = jnp.where(row >= col, mixed, mixed.T)
-    second = jnp.where(row < col, mixed, mixed.T)
-    second = jnp.where(row == col, diagonal[None], second)
-    return jnp.concatenate(
-        [jnp.concatenate([first, cross.T], axis=1), jnp.concatenate([cross, second], axis=1)], axis=0
-    )
 
 
 def summed(array, axis):
@@ -379,9 +373,8 @@
     high, low = filter_rows(top, own, bottom)
     flat = filter_columns(high, low, *sides)
     field, gram = correlate(flat, *corners, height, points)
-    total = pack(gram).reshape(-1)
-    total = summed(summed(total, "row"), "col")
-    gram = unpack(total.reshape(count // 2 + 2, count))
+    total = summed(summed(gram.reshape(-1), "row"), "col")
+    gram = total.reshape(count // 2 + 2, count)
     return tuple(orthonormal(gram, field, height, width))
 
 

time: 76.5 us -> 76.1 us (level)
  no operation moved by 1% of the time
where the time goes in v5:
time: 76.1 us; the launch traced here: 75.8 us
  blocking collectives  37.4 us (49%)
  starting transfers between devices  21.2 us (28%)
  Pallas kernels  11.5 us (15%)
  waiting for transfers between devices  2.92 us (4%)
  local copies, waits for them, and re-layouts  1.79 us (2%)
    all_to_all x2, blocking collectives, summed(): return lax.all_to_all(copies, axis, 0, 0).sum(0)  37.4 us
    ppermute x3, starting transfers between devices, swap(): second = lax.ppermute(downward, axis, down)  11.4 us
    ppermute x3, starting transfers between devices, swap(): first = lax.ppermute(upward, axis, up)  9.78 us
    pallas_call x1, Pallas kernels, orthonormal(): pl.pallas_call(basis_kernel, grid=(height // STEP,), compiler_params=pltp...  5.63 us
    pallas_call x1, Pallas kernels, filter_columns(): pl.pallas_call(columns_kernel, out_shape=shape(64 * (height + PAD), width...  2.32 us
    ppermute x3, waiting for transfers between devices, swap(): second = lax.ppermute(downward, axis, down)  2.12 us
    pallas_call x1, Pallas kernels, correlate(): pl.pallas_call(functools.partial(gram_kernel, points, height), out_shape=...  2.05 us
  transfers between devices with their start and end apart: 6, of which 3 were waited for; matrix products, arithmetic and copies ran while one was open for 0% of the time, Pallas kernels for 4%

profile of v5, /device:TPU:1, one launch (start us, length us, event | category | flops | bytes accessed | tf_op | source)
XLA Modules:
  0.0 75.8 jit_solution(1840703681893469558)
XLA Ops:
  0.6 0.0 copy-start
  0.6 1.4 %copy-done = bf16[64,96,128]{2,1,0:T(8,128)(2,1)S(1)} copy-done((bf16[64,96,128]{2,1,0:T(8,128)(2,1)S(1)}, bf16[64,96,128]{2,1,0:T(8,128)(2,1)}, u32[]{:S(2)}) %copy-start) | copy-done | bytes 1572888
  2.0 0.0 copy-start.1
  2.0 0.6 shard_map.50
  2.6 3.9 %collective-permute-start.2 = (bf16[8,96,128]{2,1,0:T(8,128)(2,1)S(1)}, bf16[8,96,128]{2,1,0:T(8,128)(2,1)S(1)}, u32[]{:S(2)}, u32[]{:S(2)}) collective-permute-start(bf16[8,96,128]{2,1,0:T(8,128)(2,1)S(1)} %get-tuple-element.14), channel_id=1, source_target_pairs={{0,1},{1,2},{2,3},{3,4},{4,5},{5,6},{6,7},{7,8},{8,9},{9,10},{10,1... | collective-permute-start | bytes 589832 | tf_op jit(solution)/shard_map/ppermute | solution.py:357
  6.6 2.1 %collective-permute-start = (bf16[8,8,16,128]{3,2,1,0:T(8,128)(2,1)S(1)}, bf16[8,8,16,128]{3,2,1,0:T(8,128)(2,1)S(1)}, u32[]{:S(2)}, u32[]{:S(2)}) collective-permute-start(bf16[8,8,16,128]{3,2,1,0:T(8,128)(2,1)S(1)} %get-tuple-element.10), channel_id=1, source_target_pairs={{0,32},{32,64},{64,96},{96,128},{128,160},{160,192},{192,224},{224... | collective-permute-start | bytes 786440 | tf_op jit(solution)/shard_map/ppermute | solution.py:357
  8.7 2.7 %collective-permute-start.1 = (bf16[8,8,16,128]{3,2,1,0:T(8,128)(2,1)S(1)}, bf16[8,8,16,128]{3,2,1,0:T(8,128)(2,1)S(1)}, u32[]{:S(2)}, u32[]{:S(2)}) collective-permute-start(bf16[8,8,16,128]{3,2,1,0:T(8,128)(2,1)S(1)} %get-tuple-element.11), channel_id=1, source_target_pairs={{32,0},{64,32},{96,64},{128,96},{160,128},{192,160},{224,192},{256... | collective-permute-start | bytes 786440 | tf_op jit(solution)/shard_map/ppermute | solution.py:358
  11.4 8.7 %collective-permute-start.3 = (bf16[8,96,128]{2,1,0:T(8,128)(2,1)S(1)}, bf16[8,96,128]{2,1,0:T(8,128)(2,1)S(1)}, u32[]{:S(2)}, u32[]{:S(2)}) collective-permute-start(bf16[8,96,128]{2,1,0:T(8,128)(2,1)S(1)} %get-tuple-element.15), channel_id=1, source_target_pairs={{1,0},{2,1},{3,2},{4,3},{5,4},{6,5},{7,6},{8,7},{9,8},{10,9},{11,1... | collective-permute-start | bytes 589832 | tf_op jit(solution)/shard_map/ppermute | solution.py:358
  20.1 0.8 %collective-permute-done.2.left = bf16[8,96,128]{2,1,0:T(8,128)(2,1)S(1)} collective-permute-done((bf16[8,96,128]{2,1,0:T(8,128)(2,1)S(1)}, bf16[8,96,128]{2,1,0:T(8,128)(2,1)S(1)}, u32[]{:S(2)}, u32[]{:S(2)}) %collective-permute-start.2) | collective-permute-done | bytes 196640 | tf_op jit(solution)/shard_map/ppermute | solution.py:357
  20.9 1.8 %collective-permute-done.3.right = bf16[8,96,128]{2,1,0:T(8,128)(2,1)S(1)} collective-permute-done((bf16[8,96,128]{2,1,0:T(8,128)(2,1)S(1)}, bf16[8,96,128]{2,1,0:T(8,128)(2,1)S(1)}, u32[]{:S(2)}, u32[]{:S(2)}) %collective-permute-start.3) | collective-permute-done | bytes 196640 | tf_op jit(solution)/shard_map/ppermute | solution.py:358
  22.7 3.7 %collective-permute-start.4 = (bf16[16,16,128]{2,1,0:T(8,128)(2,1)S(1)}, bf16[16,16,128]{2,1,0:T(8,128)(2,1)S(1)}, u32[]{:S(2)}, u32[]{:S(2)}) collective-permute-start(bf16[16,16,128]{2,1,0:T(8,128)(2,1)S(1)} %pad_maximum_fusion), channel_id=1, source_target_pairs={{0,32},{32,64},{64,96},{96,128},{128,160},{160,192},{192,224},{224... | collective-permute-start | bytes 196616 | tf_op jit(solution)/shard_map/ppermute | solution.py:357
  26.4 0.0 collective-permute-start.5
  26.4 0.0 collective-permute-done.top
  26.5 0.0 collective-permute-done.1.bottom
  26.5 1.0 %shard_map.51 = (bf16[8,8,96,128]{3,2,1,0:T(8,128)(2,1)S(1)}, bf16[8,8,96,128]{3,2,1,0:T(8,128)(2,1)S(1)}) custom-call(bf16[8,8,16,128]{3,2,1,0:T(8,128)(2,1)S(1)} %collective-permute-done.top, bf16[8,8,96,128]{3,2,1,0:T(8,128)(2,1)S(1)} %bitcast.2, bf16[8,8,16,128]{3,2,1,0:T(8,128)(2,1)S(1)} %collective-permute-done.1.bottom), custom_call_target="tpu_custom_call" | custom-call | flops 402653184 | bytes 4718592 | tf_op jit(solution)/shard_map/pallas_call | solution.py:296
  27.4 0.0 copy-done.1
  27.4 0.0 copy-start.2
  27.5 2.3 %shard_map.52.flat = f32[6656,128]{1,0:T(8,128)S(1)} custom-call(bf16[8,8,96,128]{3,2,1,0:T(8,128)(2,1)S(1)} %get-tuple-element.12.high, bf16[8,8,96,128]{3,2,1,0:T(8,128)(2,1)S(1)} %get-tuple-element.13.low, bf16[8,96,128]{2,1,0:T(8,128)(2,1)S(1)} %collective-permute-done.2.left, bf16[8,96,128]{2,1,0:T(8,128)(2,1)S(1)} %collective-permute-done.3.right, ...), custom_call_target="tpu_custom_call" | custom-call | flops 1207959552 | bytes 6291456 | tf_op jit(solution)/shard_map/pallas_call | solution.py:310
  29.8 0.0 collective-permute-done.4.top
  29.8 0.3 collective-permute-done.5.bottom
  30.1 0.0 copy-done.2
  30.1 2.0 %shard_map.53 = (bf16[128,12288]{1,0:T(8,128)(2,1)S(1)}, f32[34,64]{1,0:T(8,128)S(1)}) custom-call(f32[6656,128]{1,0:T(8,128)S(1)} %shard_map.52.flat, bf16[16,16,128]{2,1,0:T(8,128)(2,1)S(1)} %collective-permute-done.4.top, bf16[16,16,128]{2,1,0:T(8,128)(2,1)S(1)} %collective-permute-done.5.bottom, bf16[2,128,256]{2,1,0:T(8,128)(2,1)S(1)} %copy-done.2), custom_call_target="tpu_custom_call" | custom-call | tf_op jit(solution)/shard_map/pallas_call | solution.py:325
  32.2 0.1 broadcast_in_dim.6
  32.3 0.1 broadcast_in_dim.14
  32.3 17.5 %all_to_all.12 = f32[16,1,2176]{2,1,0:T(1,128)S(1)} all-to-all(f32[16,1,2176]{2,1,0:T(1,128)S(1)} %broadcast_in_dim.14), channel_id=1, replica_groups=mesh['row'=16,'col'=32] {'row'}, dimensions={0} | all-to-all | bytes 278528 | tf_op jit(solution)/shard_map/all_to_all | solution.py:350
  49.9 0.1 reduce_sum.18
  50.0 0.1 broadcast_in_dim.15
  50.1 19.8 %all_to_all.13 = f32[32,1,2176]{2,1,0:T(1,128)S(1)} all-to-all(f32[32,1,2176]{2,1,0:T(1,128)S(1)} %broadcast_in_dim.15), channel_id=1, replica_groups=mesh['row'=16,'col'=32] {'col'}, dimensions={0} | all-to-all | bytes 557056 | tf_op jit(solution)/shard_map/all_to_all | solution.py:350
  70.0 0.2 reduce_sum.19
  70.1 0.1 reshape.25.gram
  70.2 5.6 %shard_map.54 = (f32[64,96,128]{2,1,0:T(8,128)}, f32[64,64]{1,0:T(8,128)}) custom-call(f32[34,64]{1,0:T(8,128)S(1)} %reshape.25.gram, bf16[128,12288]{1,0:T(8,128)(2,1)S(1)} %get-tuple-element.17.field), custom_call_target="tpu_custom_call" | custom-call | tf_op jit(solution)/shard_map/pallas_call | solution.py:337
  (4 shorter events, 0.0 us)
Async XLA Ops:
  0.6 1.4 %copy-start = (bf16[64,96,128]{2,1,0:T(8,128)(2,1)S(1)}, bf16[64,96,128]{2,1,0:T(8,128)(2,1)}, u32[]{:S(2)}) copy-start(bf16[64,96,128]{2,1,0:T(8,128)(2,1)} %param.3) | copy-start | bytes 4718596
  2.0 25.4 %copy-start.1 = (bf16[8,256,256]{2,1,0:T(8,128)(2,1)S(1)}, bf16[8,256,256]{2,1,0:T(8,128)(2,1)}, u32[]{:S(2)}) copy-start(bf16[8,256,256]{2,1,0:T(8,128)(2,1)} %constant.6.clone.across) | copy-start | bytes 3145732
  2.6 18.3 %collective-permute-start.2 = (bf16[8,96,128]{2,1,0:T(8,128)(2,1)S(1)}, bf16[8,96,128]{2,1,0:T(8,128)(2,1)S(1)}, u32[]{:S(2)}, u32[]{:S(2)}) collective-permute-start(bf16[8,96,128]{2,1,0:T(8,128)(2,1)S(1)} %get-tuple-element.14), channel_id=1, source_target_pairs={{0,1},{1,2},{2,3},{3,4},{4,5},{5,6},{6,7},{7,8},{8,9},{9,10},{10,1... | collective-permute-start | bytes 589832 | tf_op jit(solution)/shard_map/ppermute | solution.py:357
  6.6 19.9 %collective-permute-start = (bf16[8,8,16,128]{3,2,1,0:T(8,128)(2,1)S(1)}, bf16[8,8,16,128]{3,2,1,0:T(8,128)(2,1)S(1)}, u32[]{:S(2)}, u32[]{:S(2)}) collective-permute-start(bf16[8,8,16,128]{3,2,1,0:T(8,128)(2,1)S(1)} %get-tuple-element.10), channel_id=1, source_target_pairs={{0,32},{32,64},{64,96},{96,128},{128,160},{160,192},{192,224},{224... | collective-permute-start | bytes 786440 | tf_op jit(solution)/shard_map/ppermute | solution.py:357
  8.7 17.7 %collective-permute-start.1 = (bf16[8,8,16,128]{3,2,1,0:T(8,128)(2,1)S(1)}, bf16[8,8,16,128]{3,2,1,0:T(8,128)(2,1)S(1)}, u32[]{:S(2)}, u32[]{:S(2)}) collective-permute-start(bf16[8,8,16,128]{3,2,1,0:T(8,128)(2,1)S(1)} %get-tuple-element.11), channel_id=1, source_target_pairs={{32,0},{64,32},{96,64},{128,96},{160,128},{192,160},{224,192},{256... | collective-permute-start | bytes 786440 | tf_op jit(solution)/shard_map/ppermute | solution.py:358
  11.4 11.3 %collective-permute-start.3 = (bf16[8,96,128]{2,1,0:T(8,128)(2,1)S(1)}, bf16[8,96,128]{2,1,0:T(8,128)(2,1)S(1)}, u32[]{:S(2)}, u32[]{:S(2)}) collective-permute-start(bf16[8,96,128]{2,1,0:T(8,128)(2,1)S(1)} %get-tuple-element.15), channel_id=1, source_target_pairs={{1,0},{2,1},{3,2},{4,3},{5,4},{6,5},{7,6},{8,7},{9,8},{10,9},{11,1... | collective-permute-start | bytes 589832 | tf_op jit(solution)/shard_map/ppermute | solution.py:358
  22.7 7.1 %collective-permute-start.4 = (bf16[16,16,128]{2,1,0:T(8,128)(2,1)S(1)}, bf16[16,16,128]{2,1,0:T(8,128)(2,1)S(1)}, u32[]{:S(2)}, u32[]{:S(2)}) collective-permute-start(bf16[16,16,128]{2,1,0:T(8,128)(2,1)S(1)} %pad_maximum_fusion), channel_id=1, source_target_pairs={{0,32},{32,64},{64,96},{96,128},{128,160},{160,192},{192,224},{224... | collective-permute-start | bytes 196616 | tf_op jit(solution)/shard_map/ppermute | solution.py:357
  26.4 3.7 %collective-permute-start.5 = (bf16[16,16,128]{2,1,0:T(8,128)(2,1)S(1)}, bf16[16,16,128]{2,1,0:T(8,128)(2,1)S(1)}, u32[]{:S(2)}, u32[]{:S(2)}) collective-permute-start(bf16[16,16,128]{2,1,0:T(8,128)(2,1)S(1)} %pad_maximum_fusion.1), channel_id=1, source_target_pairs={{32,0},{64,32},{96,64},{128,96},{160,128},{192,160},{224,192},{256... | collective-permute-start | bytes 196616 | tf_op jit(solution)/shard_map/ppermute | solution.py:358
  27.4 2.7 %copy-start.2 = (bf16[2,128,256]{2,1,0:T(8,128)(2,1)S(1)}, bf16[2,128,256]{2,1,0:T(8,128)(2,1)}, u32[]{:S(2)}) copy-start(bf16[2,128,256]{2,1,0:T(8,128)(2,1)} %constant.7.clone.across) | copy-start | bytes 393220
